TPU v7x, 128 devices: a whole 4x4x4 slice. The times are simulated.
128 devices in a mesh: dev: 32 (over z, x, core), rep: 4 (over y).
Axes of the slice: x: 4, y: 4, z: 4, core: 2. Of those that a mesh axis runs over, the one named last changes fastest.
Arguments:
- emb_table: float32 [131072, 160], P('dev'), may hold values from -6 to 6
- feature_ids: int32 [16384, 4, 8], P(('dev', 'rep')), may hold values from 0 to 32767
- lengths: int32 [16384, 4], P(('dev', 'rep')), may hold values from 1 to 8
- cotangent: float32 [16384, 4, 160], P(('dev', 'rep')), may hold values from -6 to 6
Outputs:
- pooled: float32 [16384, 4, 160], P(('dev', 'rep'))
- row_grads: float32 [131072, 160], P(('dev', 'rep'))
All inputs are finite; a program needn't handle non-finite values.
Results may differ from a plain program's by a relative error of at most 0.00008.
Values sent between devices are 32-bit elements; how exact they have to be, the bound alone decides.
No kernel may reach another device: no remote copies, remote signals or barrier semaphores. Data moves between devices by JAX's collectives and lax.ppermute only.
A program may use at most 128 MiB of HBM per device.

v0:
```python
import functools

import jax
import jax.numpy as jnp
from jax import lax
from jax.experimental import pallas as pl
from jax.experimental.pallas import tpu as pltpu
from jax.sharding import Mesh
from jax.sharding import PartitionSpec as P


LOW = 64
GRANT = 20 * 1024 * 1024
LANES = 128
BF = jnp.bfloat16
F32 = jnp.float32
I32 = jnp.int32
WHOLE = pl.BlockSpec(memory_space=pltpu.VMEM)
SCALARS = pl.BlockSpec(memory_space=pltpu.SMEM)


def two_parts(x):
    high = lax.reduce_precision(x, exponent_bits=8, mantissa_bits=7)
    return high.astype(BF), (x - high).astype(BF)


def estimate(width, rows, columns):
    flops = 4 * width * rows * columns
    return pl.CostEstimate(flops=flops, transcendentals=0, bytes_accessed=flops // 500)


def make_keys(base, rows_dev, ids_ref, key_low, key_high, key_count):
    bag = ids_ref.shape[1]
    own, low, lead = [], [], []
    for j in range(bag):
        ids = ids_ref[:, j, :]
        shifted = ids - base
        good = jnp.logical_and(ids >= 0, jnp.logical_and(shifted >= 0, shifted < rows_dev))
        own.append(jnp.where(good, shifted, -1))
        low.append(shifted & (LOW - 1))
        fresh = good
        for k in range(j):
            fresh = jnp.logical_and(fresh, own[k] != own[j])
        lead.append(fresh)
    deepest = jnp.zeros(own[0].shape, I32)
    for j in range(bag):
        count = jnp.ones(own[0].shape, F32)
        for k in range(j + 1, bag):
            count = count + jnp.where(own[k] == own[j], 1.0, 0.0)
        level = jnp.zeros(own[0].shape, I32)
        for k in range(j):
            level = level + jnp.where(jnp.logical_and(lead[k], low[k] == low[j]), 1, 0)
        key_low[j] = jnp.where(lead[j], low[j] + LOW * level, -1).astype(F32)
        key_high[j] = (own[j] >> (LOW.bit_length() - 1)).astype(F32)
        key_count[j] = count
        deepest = jnp.maximum(deepest, jnp.where(lead[j], level + 1, 0))
    return deepest


def spread(ref, j, source):
    return jnp.broadcast_to(ref[j, pl.ds(source, 1), :], (16, LANES)).astype(BF)


def first_layers(source, key_low, key_high, key_count):
    bag = key_low.shape[0]
    lows = [spread(key_low, j, source) for j in range(bag)]
    highs = [spread(key_high, j, source) for j in range(bag)]
    counts = [spread(key_count, j, source) for j in range(bag)]
    sub = lax.broadcasted_iota(I32, (16, LANES), 0).astype(F32)
    layers = []
    for depth in range(2):
        high_rows, count_rows = [], []
        for group in range(LOW // 16):
            place = (sub + float(LOW * depth + 16 * group)).astype(BF)
            high = jnp.full((16, LANES), -1.0, BF)
            count = jnp.zeros((16, LANES), BF)
            for j in range(bag):
                hit = lows[j] == place
                high = jnp.where(hit, highs[j], high)
                count = jnp.where(hit, counts[j], count)
            high_rows.append(high)
            count_rows.append(count)
        layers.append((jnp.concatenate(high_rows, axis=0), jnp.concatenate(count_rows, axis=0)))
    return layers


def deep_layer(source, depth, key_low, key_high, key_count):
    bag = key_low.shape[0]
    place = (lax.broadcasted_iota(I32, (LOW, LANES), 0) + LOW * depth).astype(F32)
    high = jnp.full((LOW, LANES), -1.0, F32)
    count = jnp.zeros((LOW, LANES), F32)
    for j in range(bag):
        hit = jnp.broadcast_to(key_low[j, pl.ds(source, 1), :], (LOW, LANES)) == place
        high = jnp.where(hit, jnp.broadcast_to(key_high[j, pl.ds(source, 1), :], (LOW, LANES)), high)
        count = jnp.where(hit, jnp.broadcast_to(key_count[j, pl.ds(source, 1), :], (LOW, LANES)), count)
    return high.astype(BF), count.astype(BF)


def counts_for(block, layers):
    want = jnp.asarray(block, F32).astype(BF)
    tile = jnp.zeros((LOW, LANES), BF)
    for high, count in layers:
        tile = jnp.where(high == want, count, tile)
    return tile


def pool_kernel(per_step, base_ref, ids_ref, upper_ref, lower_ref, out_ref, highs_ref, counts_ref, depth_ref,
                key_low, key_high, key_count):
    step = pl.program_id(0)
    width = out_ref.shape[1]
    rows_dev = upper_ref.shape[1]
    sources = ids_ref.shape[0]

    def build(at):
        for s in range(per_step):
            layers = first_layers(at * per_step + s, key_low, key_high, key_count)
            for depth in range(2):
                highs_ref[depth, at * per_step + s] = layers[depth][0]
                counts_ref[depth, at * per_step + s] = layers[depth][1]

    @pl.when(step == 0)
    def _():
        deepest = make_keys(base_ref[0], rows_dev, ids_ref, key_low, key_high, key_count)
        depth_ref[0] = jnp.max(deepest)

        @pl.when(depth_ref[0] > 2)
        def _():
            for s in range(sources):
                depth_ref[1 + s] = jnp.max(deepest[s : s + 1])

        build(0)

    layers = [[(highs_ref[depth, step * per_step + s], counts_ref[depth, step * per_step + s])
               for depth in range(2)] for s in range(per_step)]
    both = lambda cols: jnp.concatenate([upper_ref[:, cols], lower_ref[:, cols]], axis=0)
    chunk = 512
    total = jnp.zeros((2 * width, LANES * per_step), F32)
    for c in range(0, rows_dev, chunk):
        tile = jnp.concatenate(
            [jnp.concatenate([counts_for(c // LOW + h, layers[s]) for h in range(chunk // LOW)], axis=0)
             for s in range(per_step)], axis=1)
        total = total + jnp.dot(both(slice(c, c + chunk)), tile, preferred_element_type=F32)
    for s in range(per_step):
        cols = slice(LANES * s, LANES * (s + 1))
        out_ref[s] = total[0:width, cols] + total[width : 2 * width, cols]

    build(jnp.minimum(step + 1, sources // per_step - 1))

    @pl.when(depth_ref[0] > 2)
    def _():
        for s in range(per_step):
            source = step * per_step + s

            def deeper(depth, carry):
                extra = deep_layer(source, depth, key_low, key_high, key_count)
                wide = 512

                def add(block, value):
                    tile = jnp.concatenate([counts_for(block * (wide // LOW) + h, [extra])
                                            for h in range(wide // LOW)], axis=0)
                    return value + jnp.dot(both(pl.ds(pl.multiple_of(block * wide, wide), wide)),
                                           tile, preferred_element_type=F32)

                more = lax.fori_loop(0, rows_dev // wide, add, jnp.zeros((2 * width, LANES), F32))
                out_ref[s] += more[0:width] + more[width : 2 * width]
                return carry

            lax.fori_loop(2, depth_ref[1 + source], deeper, 0)


def pool(base, ids, parts):
    sources, bag, _ = ids.shape
    width, rows_dev = parts[0].shape
    per_step = 2
    keys = pltpu.VMEM((bag, sources, LANES), F32)
    layer = jax.ShapeDtypeStruct((2, sources, LOW, LANES), BF)
    return pl.pallas_call(
        functools.partial(pool_kernel, per_step),
        grid=(sources // per_step,),
        in_specs=[SCALARS, WHOLE, WHOLE, WHOLE],
        out_specs=[pl.BlockSpec((per_step, width, LANES), lambda i: (i, 0, 0)), WHOLE, WHOLE, SCALARS],
        out_shape=[
            jax.ShapeDtypeStruct((sources, width, LANES), F32),
            layer,
            layer,
            jax.ShapeDtypeStruct((1 + sources,), I32),
        ],
        scratch_shapes=[keys, keys, keys],
        compiler_params=pltpu.CompilerParams(dimension_semantics=("arbitrary",), vmem_limit_bytes=GRANT),
        cost_estimate=estimate(width, rows_dev, sources * LANES),
        name="pool",
    )(base, ids, *parts)


def grad_kernel(blk, steps, rows_dev, base_ref, first_ref, *refs):
    halves = [refs[0:6], refs[6:12]]
    outs, (key_low, key_high, key_count) = refs[12:-3], refs[-3:]
    half = outs[0].shape[0]
    width = 2 * half
    step = pl.program_id(0)
    start = first_ref[step // steps] + step % steps * (blk // LOW)
    together = 4
    total = jnp.zeros((2 * width, blk), F32)
    for ids_ref, upper_ref, lower_ref, highs_ref, counts_ref, depth_ref in halves:
        for s in range(0, ids_ref.shape[0], together):
            tile = jnp.concatenate(
                [jnp.concatenate([counts_for(start + h, [(highs_ref[d, s + t], counts_ref[d, s + t]) for d in range(2)])
                                  for h in range(blk // LOW)], axis=0)
                 for t in range(together)], axis=1)
            lhs = jnp.concatenate([jnp.concatenate([upper_ref[s + t], lower_ref[s + t]], axis=0)
                                   for t in range(together)], axis=1)
            total = total + lax.dot_general(lhs, tile,
                                            (((1,), (1,)), ((), ())), preferred_element_type=F32)

    def put(value, more):
        for group in range(len(outs) // 2):
            @pl.when(step // steps == group)
            def _():
                for ref, at in ((outs[2 * group], 0), (outs[2 * group + 1], half)):
                    new = value[at : at + half] + value[width + at : width + at + half]
                    ref[...] = ref[...] + new if more else new

    put(total, False)

    for ids_ref, upper_ref, lower_ref, highs_ref, counts_ref, depth_ref in halves:
        @pl.when(depth_ref[0] > 2)
        def _():
            make_keys(base_ref[0], rows_dev, ids_ref, key_low, key_high, key_count)

            def visit(s, carry):
                def deeper(depth, inner):
                    extra = deep_layer(s, depth, key_low, key_high, key_count)
                    tile = jnp.concatenate([counts_for(start + h, [extra]) for h in range(blk // LOW)], axis=0)
                    lhs = jnp.concatenate([upper_ref[s], lower_ref[s]], axis=0)
                    more = lax.dot_general(lhs, tile,
                                           (((1,), (1,)), ((), ())), preferred_element_type=F32)
                    put(more, True)
                    return inner

                return lax.fori_loop(2, depth_ref[1 + s], deeper, carry)

            lax.fori_loop(0, ids_ref.shape[0], visit, 0)


def grads(base, firsts, rows, rows_dev, own, other):
    sources, bag, _ = own[0].shape
    width = own[1].shape[1]
    blk = 256
    steps = rows // blk
    keys = pltpu.VMEM((bag, sources, LANES), F32)
    outs = [pl.BlockSpec((width // 2, blk), lambda i, g=g: (0, jnp.clip(i - g * steps, 0, steps - 1)))
            for g in range(len(firsts)) for _ in range(2)]
    each = [WHOLE, WHOLE, WHOLE, WHOLE, WHOLE, SCALARS]
    return pl.pallas_call(
        functools.partial(grad_kernel, blk, steps, rows_dev),
        grid=(steps * len(firsts),),
        in_specs=[SCALARS, SCALARS] + each + each,
        out_specs=outs,
        out_shape=[jax.ShapeDtypeStruct((width // 2, rows), F32)] * len(outs),
        scratch_shapes=[keys, keys, keys],
        compiler_params=pltpu.CompilerParams(dimension_semantics=("arbitrary",), vmem_limit_bytes=GRANT),
        cost_estimate=estimate(width, rows * len(firsts), 2 * sources * LANES),
        name="grads",
    )(base, jnp.stack(firsts).astype(I32) // LOW, *own, *other)


def to_all(x, axis):
    return lax.all_to_all(x, axis, split_axis=0, concat_axis=0, tiled=True)


def shifted(x, axis, by):
    n = lax.axis_size(axis)
    return lax.ppermute(x, axis, [(i, (i + by) % n) for i in range(n)])


def inner(emb_table, feature_ids, lengths, cotangent):
    rows_dev, width = emb_table.shape
    examples, features, bag = feature_ids.shape
    chips = lax.axis_size("x")
    cores = lax.axis_size("core")
    reps = lax.axis_size("rep")
    core = lax.axis_index("core")
    rep = lax.axis_index("rep")
    base = ((lax.axis_index("x") * cores + core) * rows_dev).astype(I32).reshape(1)

    ids_t = jnp.transpose(feature_ids, (1, 2, 0))
    lengths_t = jnp.transpose(lengths, (1, 0))
    share = 1.0 / lengths_t.astype(F32)
    slot = lax.broadcasted_iota(I32, ids_t.shape, 1)
    masked = jnp.where(slot < lengths_t[:, None, :], ids_t, -1)
    spread_ids = jnp.repeat(masked, chips * cores, axis=0)
    ids = to_all(spread_ids, ("z", "x", "core"))
    parts = two_parts(jnp.transpose(emb_table))
    ids = ids.reshape(features * chips, cores, bag, examples)
    ids_own = lax.dynamic_index_in_dim(ids, core, 1, keepdims=False)
    ids_other = lax.dynamic_index_in_dim(ids, 1 - core, 1, keepdims=False)

    scaled = jnp.transpose(cotangent, (1, 2, 0)) * share[:, None, :]
    scaled_own = to_all(jnp.repeat(scaled, chips, axis=0), ("z", "x"))
    scaled_other = shifted(scaled_own, "core", 1)

    sent, *layers_other = pool(base, ids_other, parts)
    sent = shifted(sent, "core", 1)
    kept, *layers_own = pool(base, ids_own, parts)
    pooled = to_all(kept + sent, ("z", "x")).reshape(features, chips, width, examples)
    pooled = jnp.sum(pooled, axis=1) * share[:, None, :]

    own = [ids_own, *two_parts(scaled_own), *layers_own]
    other = [ids_other, *two_parts(scaled_other), *layers_other]
    rows = rows_dev // reps

    def blocks(*ahead):
        return grads(base, [(rep + a) % reps * rows for a in ahead], rows, rows_dev, own, other)

    far_top, far_bottom = blocks(2)
    from_left = shifted(far_top, "rep", 1)
    from_right = shifted(far_bottom, "rep", -1)
    next_top, next_bottom, prev_top, prev_bottom = blocks(1, reps - 1)
    got_bottom = shifted(next_bottom, "rep", 1)
    got_top = shifted(prev_top, "rep", -1)
    got_left_top = shifted(next_top + from_left, "rep", 1)
    got_right_bottom = shifted(prev_bottom + from_right, "rep", -1)
    here_top, here_bottom = blocks(0)
    row_grads = jnp.concatenate(
        [here_top + got_top + got_left_top, here_bottom + got_bottom + got_right_bottom], axis=0
    )
    return jnp.transpose(pooled, (2, 0, 1)), jnp.transpose(row_grads)


def solution(mesh):
    devices = mesh.devices.reshape(4, 4, 2, mesh.shape["rep"])
    fine = Mesh(devices, ("z", "x", "core", "rep"))
    dev = ("z", "x", "core")
    every = ("z", "x", "core", "rep")
    return jax.shard_map(
        inner,
        mesh=fine,
        in_specs=(P(dev, None), P(every, None, None), P(every, None), P(every, None, None)),
        out_specs=(P(every, None, None), P(every, None)),
        check_vma=False,
    )
```

profile of v0, /device:TPU:33, one launch (start us, length us, event | category | flops | bytes accessed | tf_op | source)
XLA Modules:
  0.0 129.6 jit_solution(4028529658396083815)
XLA Ops:
  2.0 8.3 %all-to-all-start = ((s32[32,8,128]{2,1,0:T(8,128)}), s32[32,8,128]{2,1,0:T(8,128)S(1)}, u32[]{:S(2)}, u32[]{:S(2)}) async-start(s32[32,8,128]{2,1,0:T(8,128)} %bitcast.3), calls=%async_computation | async-start | bytes 262144 | tf_op jit(solution)/shard_map/all_to_all | solution.py:268
  12.0 4.9 %all-to-all-done = s32[32,8,128]{2,1,0:T(8,128)S(1)} async-done(((s32[32,8,128]{2,1,0:T(8,128)}), s32[32,8,128]{2,1,0:T(8,128)S(1)}, u32[]{:S(2)}, u32[]{:S(2)}) %all-to-all-start) | async-done | bytes 131104 | tf_op jit(solution)/shard_map/all_to_all | solution.py:268
  16.9 1.2 broadcast_in_dim.15
  18.2 5.3 %all-to-all-start.2 = ((f32[16,160,128]{2,1,0:T(8,128)}), f32[16,160,128]{2,1,0:T(8,128)}, u32[]{:S(2)}, u32[]{:S(2)}) async-start(f32[16,160,128]{2,1,0:T(8,128)} %bitcast.12), calls=%async_computation.2 | async-start | bytes 2621440 | tf_op jit(solution)/shard_map/all_to_all | solution.py:268
  23.4 2.2 %fusion = (bf16[160,4096]{1,0:T(8,128)(2,1)S(1)}, bf16[160,4096]{1,0:T(8,128)(2,1)S(1)}) fusion(f32[4096,160]{0,1:T(8,128)} %param.4), kind=kLoop, calls=%fused_computation.2 | loop fusion | flops 2621440 | bytes 5242880 | tf_op jit(solution)/shard_map/convert_element_type | solution.py:24
  25.6 11.3 %pool.3 = (f32[16,160,128]{2,1,0:T(8,128)}, bf16[2,16,64,128]{3,2,1,0:T(8,128)(2,1)S(1)}, bf16[2,16,64,128]{3,2,1,0:T(8,128)(2,1)S(1)}, s32[17]{0:T(128)S(1)}) custom-call(s32[1]{0:T(128)} %bitcast.base_ref, s32[16,8,128]{2,1,0:T(8,128)S(1)} %get-tuple-element.40.ids_ref.refs_6_, bf16[160,4096]{1,0:T(8,128)(2,1)S(1)} %get-tuple-element.35.upper_ref, ...), custom_call_target="tpu_custom_call" | custom-call | flops 5368709120 | bytes 10737418 | tf_op jit(solution)/shard_map/pool/pallas_call | solution.py:177
  39.2 4.0 %all-to-all-done.2 = f32[16,160,128]{2,1,0:T(8,128)} async-done(((f32[16,160,128]{2,1,0:T(8,128)}), f32[16,160,128]{2,1,0:T(8,128)}, u32[]{:S(2)}, u32[]{:S(2)}) %all-to-all-start.2) | async-done | bytes 1310752 | tf_op jit(solution)/shard_map/all_to_all | solution.py:268
  43.2 1.3 collective-permute-start.1
  44.5 10.9 %pool.2 = (f32[16,160,128]{2,1,0:T(8,128)S(1)}, bf16[2,16,64,128]{3,2,1,0:T(8,128)(2,1)S(1)}, bf16[2,16,64,128]{3,2,1,0:T(8,128)(2,1)S(1)}, s32[17]{0:T(128)S(1)}) custom-call(s32[1]{0:T(128)} %bitcast.base_ref, s32[16,8,128]{2,1,0:T(8,128)S(1)} %get-tuple-element.41.ids_ref.refs_0_, bf16[160,4096]{1,0:T(8,128)(2,1)S(1)} %get-tuple-element.35.upper_ref, ...), custom_call_target="tpu_custom_call" | custom-call | flops 5368709120 | bytes 10737418 | tf_op jit(solution)/shard_map/pool/pallas_call | solution.py:177
  55.4 1.9 %fusion.1 = (bf16[16,160,128]{2,1,0:T(8,128)(2,1)S(1)}, bf16[16,160,128]{2,1,0:T(8,128)(2,1)S(1)}) fusion(f32[16,160,128]{2,1,0:T(8,128)} %all-to-all-done.2), kind=kLoop, calls=%fused_computation.7 | loop fusion | flops 1310720 | bytes 2621440 | tf_op jit(solution)/shard_map/convert_element_type | solution.py:24
  57.4 2.6 %add.60 = f32[16,160,128]{2,1,0:T(8,128)} add(f32[16,160,128]{2,1,0:T(8,128)S(1)} %get-tuple-element.18, f32[16,160,128]{2,1,0:T(8,128)} %collective-permute-done) | non-fusion elementwise | flops 327680 | bytes 3932160 | tf_op jit(solution)/shard_map/add | solution.py:305
  59.9 5.9 %all-to-all-start.1 = ((f32[16,160,128]{2,1,0:T(8,128)}), f32[16,160,128]{2,1,0:T(8,128)}, u32[]{:S(2)}, u32[]{:S(2)}) async-start(f32[16,160,128]{2,1,0:T(8,128)} %add.60), calls=%async_computation.1 | async-start | bytes 2621440 | tf_op jit(solution)/shard_map/all_to_all | solution.py:268
  65.8 1.7 %fusion.2 = (bf16[16,160,128]{2,1,0:T(8,128)(2,1)S(1)}, bf16[16,160,128]{2,1,0:T(8,128)(2,1)S(1)}) fusion(f32[16,160,128]{2,1,0:T(8,128)} %collective-permute-done.1), kind=kLoop, calls=%fused_computation.8 | loop fusion | flops 1310720 | bytes 2621440 | tf_op jit(solution)/shard_map/convert_element_type | solution.py:24
  67.7 5.7 %grads.5 = (f32[80,1024]{1,0:T(8,128)S(1)}, f32[80,1024]{1,0:T(8,128)S(1)}) custom-call(s32[1]{0:T(128)} %bitcast.base_ref, s32[1]{0:T(128)S(6)} %select_n.52.first_ref, s32[16,8,128]{2,1,0:T(8,128)S(1)} %get-tuple-element.41.ids_ref.refs_0_, bf16[16,160,128]{2,1,0:T(8,128)(2,1)S(1)} %get-tuple-element.39.refs_1_, ...), custom_call_target="tpu_custom_call" | custom-call | flops 2684354560 | bytes 5368709 | tf_op jit(solution)/shard_map/grads/pallas_call | solution.py:254
  73.4 8.6 %collective-permute-start.6 = (f32[80,1024]{1,0:T(8,128)S(1)}, f32[80,1024]{1,0:T(8,128)S(1)}, u32[]{:S(2)}, u32[]{:S(2)}) collective-permute-start(f32[80,1024]{1,0:T(8,128)S(1)} %get-tuple-element.33), channel_id=1, source_target_pairs={{0,3},{1,0},{2,1},{3,2},{4,7},{5,4},{6,5},{7,6},{8,11},{9,8},{10,9... | collective-permute-start | bytes 983048 | tf_op jit(solution)/shard_map/ppermute | solution.py:273
  82.0 11.1 %grads.4 = (f32[80,1024]{1,0:T(8,128)S(1)}, f32[80,1024]{1,0:T(8,128)S(1)}, f32[80,1024]{1,0:T(8,128)S(1)}, f32[80,1024]{1,0:T(8,128)S(1)}) custom-call(s32[1]{0:T(128)} %bitcast.base_ref, s32[2]{0:T(128)S(1)} %and_select_fusion.first_ref, s32[16,8,128]{2,1,0:T(8,128)S(1)} %get-tuple-element.41.ids_ref.refs_0_, ...), custom_call_target="tpu_custom_call" | custom-call | flops 5368709120 | bytes 10737418 | tf_op jit(solution)/shard_map/grads/pallas_call | solution.py:254
  93.3 12.0 %collective-permute-start.2 = (f32[80,1024]{1,0:T(8,128)S(1)}, f32[80,1024]{1,0:T(8,128)}, u32[]{:S(2)}, u32[]{:S(2)}) collective-permute-start(f32[80,1024]{1,0:T(8,128)S(1)} %get-tuple-element.27), channel_id=1, source_target_pairs={{0,3},{1,0},{2,1},{3,2},{4,7},{5,4},{6,5},{7,6},{8,11},{9,8},{10,9... | collective-permute-start | bytes 983048 | tf_op jit(solution)/shard_map/ppermute | solution.py:273
  105.2 5.7 %grads.3 = (f32[80,1024]{1,0:T(8,128)S(1)}, f32[80,1024]{1,0:T(8,128)S(1)}) custom-call(s32[1]{0:T(128)} %bitcast.base_ref, s32[1]{0:T(128)S(6)} %select_n.47.first_ref, s32[16,8,128]{2,1,0:T(8,128)S(1)} %get-tuple-element.41.ids_ref.refs_0_, bf16[16,160,128]{2,1,0:T(8,128)(2,1)S(1)} %get-tuple-element.39.refs_1_, ...), custom_call_target="tpu_custom_call" | custom-call | flops 2684354560 | bytes 5368709 | tf_op jit(solution)/shard_map/grads/pallas_call | solution.py:254
  111.0 7.0 %collective-permute-start.7 = (f32[80,1024]{1,0:T(8,128)S(1)}, f32[80,1024]{1,0:T(8,128)S(1)}, u32[]{:S(2)}, u32[]{:S(2)}) collective-permute-start(f32[80,1024]{1,0:T(8,128)S(1)} %add.72), channel_id=1, source_target_pairs={{0,3},{1,0},{2,1},{3,2},{4,7},{5,4},{6,5},{7,6},{8,11},{9,8},{10,9... | collective-permute-start | bytes 983048 | tf_op jit(solution)/shard_map/ppermute | solution.py:273
  118.1 1.4 %bitcast_reduce_fusion = f32[4,160,128]{2,1,0:T(8,128)S(1)} fusion(f32[16,160,128]{2,1,0:T(8,128)} %all-to-all-done.1), kind=kLoop, calls=%fused_computation.9 | loop fusion | flops 245760 | bytes 1638400 | tf_op jit(solution)/shard_map/reduce_sum | solution.py:306
  119.5 1.0 add.69
  122.1 1.0 add_add_fusion
  123.1 4.6 %collective-permute-done.4 = f32[80,1024]{1,0:T(8,128)S(1)} collective-permute-done((f32[80,1024]{1,0:T(8,128)S(1)}, f32[80,1024]{1,0:T(8,128)S(1)}, u32[]{:S(2)}, u32[]{:S(2)}) %collective-permute-start.4) | collective-permute-done | bytes 327712 | tf_op jit(solution)/shard_map/ppermute | solution.py:273
  127.7 1.0 add_add_fusion.1
  (40 shorter events, 8.3 us)
Async XLA Ops:
  2.0 14.9 %all-to-all-start = ((s32[32,8,128]{2,1,0:T(8,128)}), s32[32,8,128]{2,1,0:T(8,128)S(1)}, u32[]{:S(2)}, u32[]{:S(2)}) async-start(s32[32,8,128]{2,1,0:T(8,128)} %bitcast.3), calls=%async_computation | async-start | bytes 262144 | tf_op jit(solution)/shard_map/all_to_all | solution.py:268
  18.2 25.0 %all-to-all-start.2 = ((f32[16,160,128]{2,1,0:T(8,128)}), f32[16,160,128]{2,1,0:T(8,128)}, u32[]{:S(2)}, u32[]{:S(2)}) async-start(f32[16,160,128]{2,1,0:T(8,128)} %bitcast.12), calls=%async_computation.2 | async-start | bytes 2621440 | tf_op jit(solution)/shard_map/all_to_all | solution.py:268
  25.6 18.9 %copy-start.8 = (s32[128,4]{0,1:T(4,128)S(1)}, s32[128,4]{0,1:T(4,128)}, u32[]{:S(2)}) copy-start(s32[128,4]{0,1:T(4,128)} %param.6) | copy-start | bytes 6148
  36.9 0.8 copy-start
  37.7 0.8 copy-start.2
  38.6 18.8 %collective-permute-start = (f32[16,160,128]{2,1,0:T(8,128)}, f32[16,160,128]{2,1,0:T(8,128)}, u32[]{:S(2)}, u32[]{:S(2)}) collective-permute-start(f32[16,160,128]{2,1,0:T(8,128)} %get-tuple-element.19), channel_id=1, source_target_pairs={{0,4},{4,0},{1,5},{5,1},{2,6},{6,2},{3,7},{7,3},{8,12},{12,8},{9,1... | collective-permute-start | bytes 3932168 | tf_op jit(solution)/shard_map/ppermute | solution.py:273
  43.2 22.6 %collective-permute-start.1 = (f32[16,160,128]{2,1,0:T(8,128)}, f32[16,160,128]{2,1,0:T(8,128)}, u32[]{:S(2)}, u32[]{:S(2)}) collective-permute-start(f32[16,160,128]{2,1,0:T(8,128)} %all-to-all-done.2), channel_id=1, source_target_pairs={{0,4},{4,0},{1,5},{5,1},{2,6},{6,2},{3,7},{7,3},{8,12},{12,8},{9,1... | collective-permute-start | bytes 3932168 | tf_op jit(solution)/shard_map/ppermute | solution.py:273
  55.4 1.9 %copy-start.4 = (bf16[2,16,64,128]{3,2,1,0:T(8,128)(2,1)}, bf16[2,16,64,128]{3,2,1,0:T(8,128)(2,1)S(1)}, u32[]{:S(2)}) copy-start(bf16[2,16,64,128]{3,2,1,0:T(8,128)(2,1)S(1)} %get-tuple-element.20.refs_3_) | copy-start | bytes 1572868
  55.4 1.9 %copy-start.6 = (bf16[2,16,64,128]{3,2,1,0:T(8,128)(2,1)}, bf16[2,16,64,128]{3,2,1,0:T(8,128)(2,1)S(1)}, u32[]{:S(2)}) copy-start(bf16[2,16,64,128]{3,2,1,0:T(8,128)(2,1)S(1)} %get-tuple-element.21.refs_4_) | copy-start | bytes 1572868
  59.9 58.1 %all-to-all-start.1 = ((f32[16,160,128]{2,1,0:T(8,128)}), f32[16,160,128]{2,1,0:T(8,128)}, u32[]{:S(2)}, u32[]{:S(2)}) async-start(f32[16,160,128]{2,1,0:T(8,128)} %add.60), calls=%async_computation.1 | async-start | bytes 2621440 | tf_op jit(solution)/shard_map/all_to_all | solution.py:268
  65.8 1.7 %copy-start.1 = (bf16[2,16,64,128]{3,2,1,0:T(8,128)(2,1)S(1)}, bf16[2,16,64,128]{3,2,1,0:T(8,128)(2,1)}, u32[]{:S(2)}) copy-start(bf16[2,16,64,128]{3,2,1,0:T(8,128)(2,1)} %copy-done) | copy-start | bytes 1572868
  65.8 1.7 %copy-start.3 = (bf16[2,16,64,128]{3,2,1,0:T(8,128)(2,1)S(1)}, bf16[2,16,64,128]{3,2,1,0:T(8,128)(2,1)}, u32[]{:S(2)}) copy-start(bf16[2,16,64,128]{3,2,1,0:T(8,128)(2,1)} %copy-done.2) | copy-start | bytes 1572868
  65.8 1.7 %copy-start.5 = (bf16[2,16,64,128]{3,2,1,0:T(8,128)(2,1)S(1)}, bf16[2,16,64,128]{3,2,1,0:T(8,128)(2,1)}, u32[]{:S(2)}) copy-start(bf16[2,16,64,128]{3,2,1,0:T(8,128)(2,1)} %copy-done.4) | copy-start | bytes 1572868
  65.8 1.9 %copy-start.7 = (bf16[2,16,64,128]{3,2,1,0:T(8,128)(2,1)S(1)}, bf16[2,16,64,128]{3,2,1,0:T(8,128)(2,1)}, u32[]{:S(2)}) copy-start(bf16[2,16,64,128]{3,2,1,0:T(8,128)(2,1)} %copy-done.6) | copy-start | bytes 1572868
  73.4 37.5 %collective-permute-start.6 = (f32[80,1024]{1,0:T(8,128)S(1)}, f32[80,1024]{1,0:T(8,128)S(1)}, u32[]{:S(2)}, u32[]{:S(2)}) collective-permute-start(f32[80,1024]{1,0:T(8,128)S(1)} %get-tuple-element.33), channel_id=1, source_target_pairs={{0,3},{1,0},{2,1},{3,2},{4,7},{5,4},{6,5},{7,6},{8,11},{9,8},{10,9... | collective-permute-start | bytes 983048 | tf_op jit(solution)/shard_map/ppermute | solution.py:273
  93.1 28.2 %collective-permute-start.5 = (f32[80,1024]{1,0:T(8,128)S(1)}, f32[80,1024]{1,0:T(8,128)}, u32[]{:S(2)}, u32[]{:S(2)}) collective-permute-start(f32[80,1024]{1,0:T(8,128)S(1)} %get-tuple-element.31), channel_id=1, source_target_pairs={{0,1},{1,2},{2,3},{3,0},{4,5},{5,6},{6,7},{7,4},{8,9},{9,10},{10,1... | collective-permute-start | bytes 983048 | tf_op jit(solution)/shard_map/ppermute | solution.py:273
  93.2 26.3 %collective-permute-start.3 = (f32[80,1024]{1,0:T(8,128)S(1)}, f32[80,1024]{1,0:T(8,128)}, u32[]{:S(2)}, u32[]{:S(2)}) collective-permute-start(f32[80,1024]{1,0:T(8,128)S(1)} %get-tuple-element.29), channel_id=1, source_target_pairs={{0,1},{1,2},{2,3},{3,0},{4,5},{5,6},{6,7},{7,4},{8,9},{9,10},{10,1... | collective-permute-start | bytes 983048 | tf_op jit(solution)/shard_map/ppermute | solution.py:273
  93.3 29.8 %collective-permute-start.2 = (f32[80,1024]{1,0:T(8,128)S(1)}, f32[80,1024]{1,0:T(8,128)}, u32[]{:S(2)}, u32[]{:S(2)}) collective-permute-start(f32[80,1024]{1,0:T(8,128)S(1)} %get-tuple-element.27), channel_id=1, source_target_pairs={{0,3},{1,0},{2,1},{3,2},{4,7},{5,4},{6,5},{7,6},{8,11},{9,8},{10,9... | collective-permute-start | bytes 983048 | tf_op jit(solution)/shard_map/ppermute | solution.py:273
  111.0 11.0 %collective-permute-start.7 = (f32[80,1024]{1,0:T(8,128)S(1)}, f32[80,1024]{1,0:T(8,128)S(1)}, u32[]{:S(2)}, u32[]{:S(2)}) collective-permute-start(f32[80,1024]{1,0:T(8,128)S(1)} %add.72), channel_id=1, source_target_pairs={{0,3},{1,0},{2,1},{3,2},{4,7},{5,4},{6,5},{7,6},{8,11},{9,8},{10,9... | collective-permute-start | bytes 983048 | tf_op jit(solution)/shard_map/ppermute | solution.py:273
  120.5 7.2 %collective-permute-start.4 = (f32[80,1024]{1,0:T(8,128)S(1)}, f32[80,1024]{1,0:T(8,128)S(1)}, u32[]{:S(2)}, u32[]{:S(2)}) collective-permute-start(f32[80,1024]{1,0:T(8,128)S(1)} %add.69), channel_id=1, source_target_pairs={{0,1},{1,2},{2,3},{3,0},{4,5},{5,6},{6,7},{7,4},{8,9},{9,10},{10,1... | collective-permute-start | bytes 983048 | tf_op jit(solution)/shard_map/ppermute | solution.py:273
where the time goes:
time: 130 us
  starting transfers between devices  49.2 us (38%)
  Pallas kernels  44.7 us (34%)
  other arithmetic  17 us (13%)
  waiting for transfers between devices  14.2 us (11%)
  local copies, waits for them, and re-layouts  3.72 us (3%)
    ppermute x8, starting transfers between devices, shifted(): return lax.ppermute(x, axis, [(i, (i + by) % n) for i in range(n)])  29.7 us
    pallas_call x3, Pallas kernels, grads(): pl.pallas_call(functools.partial(grad_kernel, blk, steps, rows_dev), grid...  22.5 us
    pallas_call x2, Pallas kernels, pool(): pl.pallas_call(functools.partial(pool_kernel, per_step), grid=(sources //...  22.2 us
    all_to_all x3, starting transfers between devices, to_all(): return lax.all_to_all(x, axis, split_axis=0, concat_axis=0, tiled=True)  19.4 us
    all_to_all x3, waiting for transfers between devices, to_all(): return lax.all_to_all(x, axis, split_axis=0, concat_axis=0, tiled=True)  8.85 us
    convert_element_type x3, other arithmetic, two_parts(): return (high.astype(BF), (x - high).astype(BF))  5.74 us
    ppermute x8, waiting for transfers between devices, shifted(): return lax.ppermute(x, axis, [(i, (i + by) % n) for i in range(n)])  5.35 us
  transfers between devices with their start and end apart: 11, of which 4 were waited for; matrix products, arithmetic and copies ran while one was open for 11% of the time, Pallas kernels for 35%

commit v1 on v0

--- a/solution.py
+++ b/solution.py
@@ -10,6 +10,8 @@
 
 
 LOW = 64
+CHUNK = 256
+TOGETHER = 2
 GRANT = 20 * 1024 * 1024
 LANES = 128
 BF = jnp.bfloat16
@@ -133,7 +135,7 @@
     layers = [[(highs_ref[depth, step * per_step + s], counts_ref[depth, step * per_step + s])
                for depth in range(2)] for s in range(per_step)]
     both = lambda cols: jnp.concatenate([upper_ref[:, cols], lower_ref[:, cols]], axis=0)
-    chunk = 512
+    chunk = CHUNK
     total = jnp.zeros((2 * width, LANES * per_step), F32)
     for c in range(0, rows_dev, chunk):
         tile = jnp.concatenate(
@@ -172,37 +174,38 @@
     sources, bag, _ = ids.shape
     width, rows_dev = parts[0].shape
     per_step = 2
-    keys = pltpu.VMEM((bag, sources, LANES), F32)
+    keys = jax.ShapeDtypeStruct((bag, sources, LANES), F32)
     layer = jax.ShapeDtypeStruct((2, sources, LOW, LANES), BF)
     return pl.pallas_call(
         functools.partial(pool_kernel, per_step),
         grid=(sources // per_step,),
         in_specs=[SCALARS, WHOLE, WHOLE, WHOLE],
-        out_specs=[pl.BlockSpec((per_step, width, LANES), lambda i: (i, 0, 0)), WHOLE, WHOLE, SCALARS],
+        out_specs=[pl.BlockSpec((per_step, width, LANES), lambda i: (i, 0, 0)), WHOLE, WHOLE, SCALARS, WHOLE, WHOLE, WHOLE],
         out_shape=[
             jax.ShapeDtypeStruct((sources, width, LANES), F32),
             layer,
             layer,
             jax.ShapeDtypeStruct((1 + sources,), I32),
+            keys,
+            keys,
+            keys,
         ],
-        scratch_shapes=[keys, keys, keys],
         compiler_params=pltpu.CompilerParams(dimension_semantics=("arbitrary",), vmem_limit_bytes=GRANT),
         cost_estimate=estimate(width, rows_dev, sources * LANES),
         name="pool",
     )(base, ids, *parts)
 
 
-def grad_kernel(blk, steps, rows_dev, base_ref, first_ref, *refs):
-    halves = [refs[0:6], refs[6:12]]
-    outs, (key_low, key_high, key_count) = refs[12:-3], refs[-3:]
+def grad_kernel(blk, steps, first_ref, *refs):
+    halves, outs = [refs[0:8], refs[8:16]], refs[16:]
     half = outs[0].shape[0]
     width = 2 * half
     step = pl.program_id(0)
     start = first_ref[step // steps] + step % steps * (blk // LOW)
-    together = 4
+    together = TOGETHER
     total = jnp.zeros((2 * width, blk), F32)
-    for ids_ref, upper_ref, lower_ref, highs_ref, counts_ref, depth_ref in halves:
-        for s in range(0, ids_ref.shape[0], together):
+    for upper_ref, lower_ref, highs_ref, counts_ref, depth_ref, *keys in halves:
+        for s in range(0, upper_ref.shape[0], together):
             tile = jnp.concatenate(
                 [jnp.concatenate([counts_for(start + h, [(highs_ref[d, s + t], counts_ref[d, s + t]) for d in range(2)])
                                   for h in range(blk // LOW)], axis=0)
@@ -222,14 +225,12 @@
 
     put(total, False)
 
-    for ids_ref, upper_ref, lower_ref, highs_ref, counts_ref, depth_ref in halves:
+    for upper_ref, lower_ref, highs_ref, counts_ref, depth_ref, *keys in halves:
         @pl.when(depth_ref[0] > 2)
         def _():
-            make_keys(base_ref[0], rows_dev, ids_ref, key_low, key_high, key_count)
-
             def visit(s, carry):
                 def deeper(depth, inner):
-                    extra = deep_layer(s, depth, key_low, key_high, key_count)
+                    extra = deep_layer(s, depth, *keys)
                     tile = jnp.concatenate([counts_for(start + h, [extra]) for h in range(blk // LOW)], axis=0)
                     lhs = jnp.concatenate([upper_ref[s], lower_ref[s]], axis=0)
                     more = lax.dot_general(lhs, tile,
@@ -239,29 +240,26 @@
 
                 return lax.fori_loop(2, depth_ref[1 + s], deeper, carry)
 
-            lax.fori_loop(0, ids_ref.shape[0], visit, 0)
-
-
-def grads(base, firsts, rows, rows_dev, own, other):
-    sources, bag, _ = own[0].shape
-    width = own[1].shape[1]
+            lax.fori_loop(0, upper_ref.shape[0], visit, 0)
+
+
+def grads(firsts, rows, own, other):
+    sources, width, _ = own[0].shape
     blk = 256
     steps = rows // blk
-    keys = pltpu.VMEM((bag, sources, LANES), F32)
     outs = [pl.BlockSpec((width // 2, blk), lambda i, g=g: (0, jnp.clip(i - g * steps, 0, steps - 1)))
             for g in range(len(firsts)) for _ in range(2)]
-    each = [WHOLE, WHOLE, WHOLE, WHOLE, WHOLE, SCALARS]
+    each = [WHOLE, WHOLE, WHOLE, WHOLE, SCALARS, WHOLE, WHOLE, WHOLE]
     return pl.pallas_call(
-        functools.partial(grad_kernel, blk, steps, rows_dev),
+        functools.partial(grad_kernel, blk, steps),
         grid=(steps * len(firsts),),
-        in_specs=[SCALARS, SCALARS] + each + each,
+        in_specs=[SCALARS] + each + each,
         out_specs=outs,
         out_shape=[jax.ShapeDtypeStruct((width // 2, rows), F32)] * len(outs),
-        scratch_shapes=[keys, keys, keys],
         compiler_params=pltpu.CompilerParams(dimension_semantics=("arbitrary",), vmem_limit_bytes=GRANT),
         cost_estimate=estimate(width, rows * len(firsts), 2 * sources * LANES),
         name="grads",
-    )(base, jnp.stack(firsts).astype(I32) // LOW, *own, *other)
+    )(jnp.stack(firsts).astype(I32) // LOW, *own, *other)
 
 
 def to_all(x, axis):
@@ -296,7 +294,8 @@
     ids_other = lax.dynamic_index_in_dim(ids, 1 - core, 1, keepdims=False)
 
     scaled = jnp.transpose(cotangent, (1, 2, 0)) * share[:, None, :]
-    scaled_own = to_all(jnp.repeat(scaled, chips, axis=0), ("z", "x"))
+    spread_cot = jnp.repeat(scaled, chips, axis=0)
+    scaled_own = to_all(spread_cot, ("z", "x"))
     scaled_other = shifted(scaled_own, "core", 1)
 
     sent, *layers_other = pool(base, ids_other, parts)
@@ -305,12 +304,12 @@
     pooled = to_all(kept + sent, ("z", "x")).reshape(features, chips, width, examples)
     pooled = jnp.sum(pooled, axis=1) * share[:, None, :]
 
-    own = [ids_own, *two_parts(scaled_own), *layers_own]
-    other = [ids_other, *two_parts(scaled_other), *layers_other]
+    own = [*two_parts(scaled_own), *layers_own]
+    other = [*two_parts(scaled_other), *layers_other]
     rows = rows_dev // reps
 
     def blocks(*ahead):
-        return grads(base, [(rep + a) % reps * rows for a in ahead], rows, rows_dev, own, other)
+        return grads([(rep + a) % reps * rows for a in ahead], rows, own, other)
 
     far_top, far_bottom = blocks(2)
     from_left = shifted(far_top, "rep", 1)

time: 130 us -> 120 us (0.923)
  the two profiles are of different devices: /device:TPU:33 before, /device:TPU:0 now
where the time goes in v1:
time: 120 us
  Pallas kernels  45.3 us (38%)
  waiting for transfers between devices  26.7 us (22%)
  starting transfers between devices  25.9 us (22%)
  other arithmetic  17 us (14%)
  local copies, waits for them, and re-layouts  3.69 us (3%)
    pallas_call x3, Pallas kernels, grads(): pl.pallas_call(functools.partial(grad_kernel, blk, steps), grid=(steps *...  23 us
    pallas_call x2, Pallas kernels, pool(): pl.pallas_call(functools.partial(pool_kernel, per_step), grid=(sources //...  22.3 us
    all_to_all x3, starting transfers between devices, to_all(): return lax.all_to_all(x, axis, split_axis=0, concat_axis=0, tiled=True)  17.1 us
    ppermute x8, waiting for transfers between devices, shifted(): return lax.ppermute(x, axis, [(i, (i + by) % n) for i in range(n)])  13.9 us
    all_to_all x3, waiting for transfers between devices, to_all(): return lax.all_to_all(x, axis, split_axis=0, concat_axis=0, tiled=True)  12.8 us
    ppermute x8, starting transfers between devices, shifted(): return lax.ppermute(x, axis, [(i, (i + by) % n) for i in range(n)])  8.84 us
    convert_element_type x3, other arithmetic, two_parts(): return (high.astype(BF), (x - high).astype(BF))  5.77 us
    add x1, other arithmetic, inner(): kept + sent  2.57 us
  transfers between devices with their start and end apart: 11, of which 4 were waited for; matrix products, arithmetic and copies ran while one was open for 12% of the time, Pallas kernels for 38%

profile of v1, /device:TPU:0, one launch (start us, length us, event | category | flops | bytes accessed | tf_op | source)
XLA Modules:
  0.0 119.5 jit_solution(9279071869338221921)
XLA Ops:
  2.0 8.3 %all-to-all-start = ((s32[32,8,128]{2,1,0:T(8,128)}), s32[32,8,128]{2,1,0:T(8,128)S(1)}, u32[]{:S(2)}, u32[]{:S(2)}) async-start(s32[32,8,128]{2,1,0:T(8,128)} %bitcast.3), calls=%async_computation | async-start | bytes 262144 | tf_op jit(solution)/shard_map/all_to_all | solution.py:266
  12.0 6.1 %all-to-all-done = s32[32,8,128]{2,1,0:T(8,128)S(1)} async-done(((s32[32,8,128]{2,1,0:T(8,128)}), s32[32,8,128]{2,1,0:T(8,128)S(1)}, u32[]{:S(2)}, u32[]{:S(2)}) %all-to-all-start) | async-done | bytes 131104 | tf_op jit(solution)/shard_map/all_to_all | solution.py:266
  18.1 1.2 %broadcast_in_dim.15 = f32[4,4,160,128]{3,2,1,0:T(8,128)} broadcast(f32[4,160,128]{2,1,0:T(8,128)S(1)} %bitcast_multiply_fusion), dimensions={0,2,3} | broadcast | bytes 1638400 | tf_op jit(solution)/shard_map/broadcast_in_dim | solution.py:297
  19.3 4.4 %all-to-all-start.2 = ((f32[16,160,128]{2,1,0:T(8,128)}), f32[16,160,128]{2,1,0:T(8,128)}, u32[]{:S(2)}, u32[]{:S(2)}) async-start(f32[16,160,128]{2,1,0:T(8,128)} %bitcast.12), calls=%async_computation.2 | async-start | bytes 2621440 | tf_op jit(solution)/shard_map/all_to_all | solution.py:266
  23.7 2.2 %fusion = (bf16[160,4096]{1,0:T(8,128)(2,1)S(1)}, bf16[160,4096]{1,0:T(8,128)(2,1)S(1)}) fusion(f32[4096,160]{0,1:T(8,128)} %param.4), kind=kLoop, calls=%fused_computation.2 | loop fusion | flops 2621440 | bytes 5242880 | tf_op jit(solution)/shard_map/convert_element_type | solution.py:26
  25.9 11.4 %pool.3 = (f32[16,160,128]{2,1,0:T(8,128)}, bf16[2,16,64,128]{3,2,1,0:T(8,128)(2,1)S(1)}, bf16[2,16,64,128]{3,2,1,0:T(8,128)(2,1)S(1)}, s32[17]{0:T(128)S(1)}, f...) custom-call(s32[1]{0:T(128)} %bitcast.base_ref, ...), custom_call_target="tpu_custom_call" | custom-call | flops 5368709120 | bytes 10737418 | tf_op jit(solution)/shard_map/pool/pallas_call | solution.py:179
  39.1 6.7 %all-to-all-done.2 = f32[16,160,128]{2,1,0:T(8,128)} async-done(((f32[16,160,128]{2,1,0:T(8,128)}), f32[16,160,128]{2,1,0:T(8,128)}, u32[]{:S(2)}, u32[]{:S(2)}) %all-to-all-start.2) | async-done | bytes 1310752 | tf_op jit(solution)/shard_map/all_to_all | solution.py:266
  45.9 10.8 %pool.2 = (f32[16,160,128]{2,1,0:T(8,128)S(1)}, bf16[2,16,64,128]{3,2,1,0:T(8,128)(2,1)S(1)}, bf16[2,16,64,128]{3,2,1,0:T(8,128)(2,1)S(1)}, s32[17]{0:T(128)S(1)...) custom-call(s32[1]{0:T(128)} %bitcast.base_ref, ...), custom_call_target="tpu_custom_call" | custom-call | flops 5368709120 | bytes 10737418 | tf_op jit(solution)/shard_map/pool/pallas_call | solution.py:179
  56.7 1.9 %fusion.1 = (bf16[16,160,128]{2,1,0:T(8,128)(2,1)S(1)}, bf16[16,160,128]{2,1,0:T(8,128)(2,1)S(1)}) fusion(f32[16,160,128]{2,1,0:T(8,128)} %all-to-all-done.2), kind=kLoop, calls=%fused_computation.7 | loop fusion | flops 1310720 | bytes 2621440 | tf_op jit(solution)/shard_map/convert_element_type | solution.py:26
  58.7 2.6 %add.60 = f32[16,160,128]{2,1,0:T(8,128)} add(f32[16,160,128]{2,1,0:T(8,128)S(1)} %get-tuple-element.24, f32[16,160,128]{2,1,0:T(8,128)} %collective-permute-done) | non-fusion elementwise | flops 327680 | bytes 3932160 | tf_op jit(solution)/shard_map/add | solution.py:304
  61.3 4.4 %all-to-all-start.1 = ((f32[16,160,128]{2,1,0:T(8,128)}), f32[16,160,128]{2,1,0:T(8,128)}, u32[]{:S(2)}, u32[]{:S(2)}) async-start(f32[16,160,128]{2,1,0:T(8,128)} %add.60), calls=%async_computation.1 | async-start | bytes 2621440 | tf_op jit(solution)/shard_map/all_to_all | solution.py:266
  65.8 1.7 %fusion.2 = (bf16[16,160,128]{2,1,0:T(8,128)(2,1)S(1)}, bf16[16,160,128]{2,1,0:T(8,128)(2,1)S(1)}) fusion(f32[16,160,128]{2,1,0:T(8,128)} %collective-permute-done.1), kind=kLoop, calls=%fused_computation.8 | loop fusion | flops 1310720 | bytes 2621440 | tf_op jit(solution)/shard_map/convert_element_type | solution.py:26
  67.6 5.8 %grads.5 = (f32[80,1024]{1,0:T(8,128)S(1)}, f32[80,1024]{1,0:T(8,128)S(1)}) custom-call(s32[1]{0:T(128)S(6)} %select_n.52.first_ref, bf16[16,160,128]{2,1,0:T(8,128)(2,1)S(1)} %get-tuple-element.51.refs_0_, bf16[16,160,128]{2,1,0:T(8,128)(2,1)S(1)} %get-tuple-element.50.refs_1_, bf16[2,16,64,128]{3,2,1,0:T(8,128)(2,1)S(1)} %copy-done.5, ...), custom_call_target="tpu_custom_call" | custom-call | flops 2684354560 | bytes 5368709 | tf_op jit(solution)/shard_map/grads/pallas_call | solution.py:253
  73.5 3.1 %collective-permute-start.6 = (f32[80,1024]{1,0:T(8,128)S(1)}, f32[80,1024]{1,0:T(8,128)S(1)}, u32[]{:S(2)}, u32[]{:S(2)}) collective-permute-start(f32[80,1024]{1,0:T(8,128)S(1)} %get-tuple-element.45), channel_id=1, source_target_pairs={{0,3},{1,0},{2,1},{3,2},{4,7},{5,4},{6,5},{7,6},{8,11},{9,8},{10,9... | collective-permute-start | bytes 983048 | tf_op jit(solution)/shard_map/ppermute | solution.py:271
  76.5 11.4 %grads.4 = (f32[80,1024]{1,0:T(8,128)S(1)}, f32[80,1024]{1,0:T(8,128)S(1)}, f32[80,1024]{1,0:T(8,128)S(1)}, f32[80,1024]{1,0:T(8,128)S(1)}) custom-call(s32[2]{0:T(128)S(1)} %and_select_fusion.first_ref, bf16[16,160,128]{2,1,0:T(8,128)(2,1)S(1)} %get-tuple-element.51.refs_0_, bf16[16,160,128]{2,1,0:T(8,128)(2,1)S(1)} %get-tuple-element.50.refs_1_, ...), custom_call_target="tpu_custom_call" | custom-call | flops 5368709120 | bytes 10737418 | tf_op jit(solution)/shard_map/grads/pallas_call | solution.py:253
  88.7 2.7 %collective-permute-start.2 = (f32[80,1024]{1,0:T(8,128)S(1)}, f32[80,1024]{1,0:T(8,128)}, u32[]{:S(2)}, u32[]{:S(2)}) collective-permute-start(f32[80,1024]{1,0:T(8,128)S(1)} %get-tuple-element.39), channel_id=1, source_target_pairs={{0,3},{1,0},{2,1},{3,2},{4,7},{5,4},{6,5},{7,6},{8,11},{9,8},{10,9... | collective-permute-start | bytes 983048 | tf_op jit(solution)/shard_map/ppermute | solution.py:271
  91.5 5.8 %grads.3 = (f32[80,1024]{1,0:T(8,128)S(1)}, f32[80,1024]{1,0:T(8,128)S(1)}) custom-call(s32[1]{0:T(128)S(6)} %select_n.47.first_ref, bf16[16,160,128]{2,1,0:T(8,128)(2,1)S(1)} %get-tuple-element.51.refs_0_, bf16[16,160,128]{2,1,0:T(8,128)(2,1)S(1)} %get-tuple-element.50.refs_1_, bf16[2,16,64,128]{3,2,1,0:T(8,128)(2,1)S(1)} %copy-done.5, ...), custom_call_target="tpu_custom_call" | custom-call | flops 2684354560 | bytes 5368709 | tf_op jit(solution)/shard_map/grads/pallas_call | solution.py:253
  97.4 2.0 %collective-permute-start.7 = (f32[80,1024]{1,0:T(8,128)S(1)}, f32[80,1024]{1,0:T(8,128)S(1)}, u32[]{:S(2)}, u32[]{:S(2)}) collective-permute-start(f32[80,1024]{1,0:T(8,128)S(1)} %add.72), channel_id=1, source_target_pairs={{0,3},{1,0},{2,1},{3,2},{4,7},{5,4},{6,5},{7,6},{8,11},{9,8},{10,9... | collective-permute-start | bytes 983048 | tf_op jit(solution)/shard_map/ppermute | solution.py:271
  99.4 1.4 %bitcast_reduce_fusion = f32[4,160,128]{2,1,0:T(8,128)S(1)} fusion(f32[16,160,128]{2,1,0:T(8,128)} %all-to-all-done.1), kind=kLoop, calls=%fused_computation.9 | loop fusion | flops 245760 | bytes 1638400 | tf_op jit(solution)/shard_map/reduce_sum | solution.py:305
  100.8 5.5 %collective-permute-done.3 = f32[80,1024]{1,0:T(8,128)} collective-permute-done((f32[80,1024]{1,0:T(8,128)S(1)}, f32[80,1024]{1,0:T(8,128)}, u32[]{:S(2)}, u32[]{:S(2)}) %collective-permute-start.3) | collective-permute-done | bytes 327712 | tf_op jit(solution)/shard_map/ppermute | solution.py:271
  106.3 1.0 add.69
  108.2 1.0 add_add_fusion
  109.2 8.4 %collective-permute-done.4 = f32[80,1024]{1,0:T(8,128)S(1)} collective-permute-done((f32[80,1024]{1,0:T(8,128)S(1)}, f32[80,1024]{1,0:T(8,128)S(1)}, u32[]{:S(2)}, u32[]{:S(2)}) %collective-permute-start.4) | collective-permute-done | bytes 327712 | tf_op jit(solution)/shard_map/ppermute | solution.py:271
  117.6 1.0 add_add_fusion.1
  (48 shorter events, 7.7 us)
Async XLA Ops:
  2.0 16.1 %all-to-all-start = ((s32[32,8,128]{2,1,0:T(8,128)}), s32[32,8,128]{2,1,0:T(8,128)S(1)}, u32[]{:S(2)}, u32[]{:S(2)}) async-start(s32[32,8,128]{2,1,0:T(8,128)} %bitcast.3), calls=%async_computation | async-start | bytes 262144 | tf_op jit(solution)/shard_map/all_to_all | solution.py:266
  19.3 26.5 %all-to-all-start.2 = ((f32[16,160,128]{2,1,0:T(8,128)}), f32[16,160,128]{2,1,0:T(8,128)}, u32[]{:S(2)}, u32[]{:S(2)}) async-start(f32[16,160,128]{2,1,0:T(8,128)} %bitcast.12), calls=%async_computation.2 | async-start | bytes 2621440 | tf_op jit(solution)/shard_map/all_to_all | solution.py:266
  25.9 20.0 %copy-start.12 = (s32[128,4]{0,1:T(4,128)S(1)}, s32[128,4]{0,1:T(4,128)}, u32[]{:S(2)}) copy-start(s32[128,4]{0,1:T(4,128)} %param.6) | copy-start | bytes 6148
  37.3 0.8 copy-start
  38.1 0.8 copy-start.2
  38.9 19.8 %collective-permute-start = (f32[16,160,128]{2,1,0:T(8,128)}, f32[16,160,128]{2,1,0:T(8,128)}, u32[]{:S(2)}, u32[]{:S(2)}) collective-permute-start(f32[16,160,128]{2,1,0:T(8,128)} %get-tuple-element.25), channel_id=1, source_target_pairs={{0,4},{4,0},{1,5},{5,1},{2,6},{6,2},{3,7},{7,3},{8,12},{12,8},{9,1... | collective-permute-start | bytes 3932168 | tf_op jit(solution)/shard_map/ppermute | solution.py:271
  45.8 20.0 %collective-permute-start.1 = (f32[16,160,128]{2,1,0:T(8,128)}, f32[16,160,128]{2,1,0:T(8,128)}, u32[]{:S(2)}, u32[]{:S(2)}) collective-permute-start(f32[16,160,128]{2,1,0:T(8,128)} %all-to-all-done.2), channel_id=1, source_target_pairs={{0,4},{4,0},{1,5},{5,1},{2,6},{6,2},{3,7},{7,3},{8,12},{12,8},{9,1... | collective-permute-start | bytes 3932168 | tf_op jit(solution)/shard_map/ppermute | solution.py:271
  56.7 2.0 %copy-start.4 = (bf16[2,16,64,128]{3,2,1,0:T(8,128)(2,1)}, bf16[2,16,64,128]{3,2,1,0:T(8,128)(2,1)S(1)}, u32[]{:S(2)}) copy-start(bf16[2,16,64,128]{3,2,1,0:T(8,128)(2,1)S(1)} %get-tuple-element.26.refs_2_) | copy-start | bytes 1572868
  56.7 2.0 %copy-start.6 = (bf16[2,16,64,128]{3,2,1,0:T(8,128)(2,1)}, bf16[2,16,64,128]{3,2,1,0:T(8,128)(2,1)S(1)}, u32[]{:S(2)}) copy-start(bf16[2,16,64,128]{3,2,1,0:T(8,128)(2,1)S(1)} %get-tuple-element.27.refs_3_) | copy-start | bytes 1572868
  56.7 2.0 %copy-start.8 = (f32[8,16,128]{2,1,0:T(8,128)}, f32[8,16,128]{2,1,0:T(8,128)S(1)}, u32[]{:S(2)}) copy-start(f32[8,16,128]{2,1,0:T(8,128)S(1)} %get-tuple-element.30.refs_6_) | copy-start | bytes 196612
  56.7 2.0 %copy-start.10 = (f32[8,16,128]{2,1,0:T(8,128)}, f32[8,16,128]{2,1,0:T(8,128)S(1)}, u32[]{:S(2)}) copy-start(f32[8,16,128]{2,1,0:T(8,128)S(1)} %get-tuple-element.31.refs_7_) | copy-start | bytes 196612
  61.3 38.1 %all-to-all-start.1 = ((f32[16,160,128]{2,1,0:T(8,128)}), f32[16,160,128]{2,1,0:T(8,128)}, u32[]{:S(2)}, u32[]{:S(2)}) async-start(f32[16,160,128]{2,1,0:T(8,128)} %add.60), calls=%async_computation.1 | async-start | bytes 2621440 | tf_op jit(solution)/shard_map/all_to_all | solution.py:266
  65.7 1.8 %copy-start.1 = (bf16[2,16,64,128]{3,2,1,0:T(8,128)(2,1)S(1)}, bf16[2,16,64,128]{3,2,1,0:T(8,128)(2,1)}, u32[]{:S(2)}) copy-start(bf16[2,16,64,128]{3,2,1,0:T(8,128)(2,1)} %copy-done) | copy-start | bytes 1572868
  65.7 1.8 %copy-start.3 = (bf16[2,16,64,128]{3,2,1,0:T(8,128)(2,1)S(1)}, bf16[2,16,64,128]{3,2,1,0:T(8,128)(2,1)}, u32[]{:S(2)}) copy-start(bf16[2,16,64,128]{3,2,1,0:T(8,128)(2,1)} %copy-done.2) | copy-start | bytes 1572868
  65.7 1.8 %copy-start.5 = (bf16[2,16,64,128]{3,2,1,0:T(8,128)(2,1)S(1)}, bf16[2,16,64,128]{3,2,1,0:T(8,128)(2,1)}, u32[]{:S(2)}) copy-start(bf16[2,16,64,128]{3,2,1,0:T(8,128)(2,1)} %copy-done.4) | copy-start | bytes 1572868
  65.7 1.9 %copy-start.7 = (bf16[2,16,64,128]{3,2,1,0:T(8,128)(2,1)S(1)}, bf16[2,16,64,128]{3,2,1,0:T(8,128)(2,1)}, u32[]{:S(2)}) copy-start(bf16[2,16,64,128]{3,2,1,0:T(8,128)(2,1)} %copy-done.6) | copy-start | bytes 1572868
  65.7 1.9 %copy-start.9 = (f32[8,16,128]{2,1,0:T(8,128)S(1)}, f32[8,16,128]{2,1,0:T(8,128)}, u32[]{:S(2)}) copy-start(f32[8,16,128]{2,1,0:T(8,128)} %copy-done.8) | copy-start | bytes 196612
  65.7 1.9 %copy-start.11 = (f32[8,16,128]{2,1,0:T(8,128)S(1)}, f32[8,16,128]{2,1,0:T(8,128)}, u32[]{:S(2)}) copy-start(f32[8,16,128]{2,1,0:T(8,128)} %copy-done.10) | copy-start | bytes 196612
  73.5 23.9 %collective-permute-start.6 = (f32[80,1024]{1,0:T(8,128)S(1)}, f32[80,1024]{1,0:T(8,128)S(1)}, u32[]{:S(2)}, u32[]{:S(2)}) collective-permute-start(f32[80,1024]{1,0:T(8,128)S(1)} %get-tuple-element.45), channel_id=1, source_target_pairs={{0,3},{1,0},{2,1},{3,2},{4,7},{5,4},{6,5},{7,6},{8,11},{9,8},{10,9... | collective-permute-start | bytes 983048 | tf_op jit(solution)/shard_map/ppermute | solution.py:271
  87.9 20.3 %collective-permute-start.5 = (f32[80,1024]{1,0:T(8,128)S(1)}, f32[80,1024]{1,0:T(8,128)}, u32[]{:S(2)}, u32[]{:S(2)}) collective-permute-start(f32[80,1024]{1,0:T(8,128)S(1)} %get-tuple-element.43), channel_id=1, source_target_pairs={{0,1},{1,2},{2,3},{3,0},{4,5},{5,6},{6,7},{7,4},{8,9},{9,10},{10,1... | collective-permute-start | bytes 983048 | tf_op jit(solution)/shard_map/ppermute | solution.py:271
  88.2 18.2 %collective-permute-start.3 = (f32[80,1024]{1,0:T(8,128)S(1)}, f32[80,1024]{1,0:T(8,128)}, u32[]{:S(2)}, u32[]{:S(2)}) collective-permute-start(f32[80,1024]{1,0:T(8,128)S(1)} %get-tuple-element.41), channel_id=1, source_target_pairs={{0,1},{1,2},{2,3},{3,0},{4,5},{5,6},{6,7},{7,4},{8,9},{9,10},{10,1... | collective-permute-start | bytes 983048 | tf_op jit(solution)/shard_map/ppermute | solution.py:271
  88.7 20.5 %collective-permute-start.2 = (f32[80,1024]{1,0:T(8,128)S(1)}, f32[80,1024]{1,0:T(8,128)}, u32[]{:S(2)}, u32[]{:S(2)}) collective-permute-start(f32[80,1024]{1,0:T(8,128)S(1)} %get-tuple-element.39), channel_id=1, source_target_pairs={{0,3},{1,0},{2,1},{3,2},{4,7},{5,4},{6,5},{7,6},{8,11},{9,8},{10,9... | collective-permute-start | bytes 983048 | tf_op jit(solution)/shard_map/ppermute | solution.py:271
  97.4 10.8 %collective-permute-start.7 = (f32[80,1024]{1,0:T(8,128)S(1)}, f32[80,1024]{1,0:T(8,128)S(1)}, u32[]{:S(2)}, u32[]{:S(2)}) collective-permute-start(f32[80,1024]{1,0:T(8,128)S(1)} %add.72), channel_id=1, source_target_pairs={{0,3},{1,0},{2,1},{3,2},{4,7},{5,4},{6,5},{7,6},{8,11},{9,8},{10,9... | collective-permute-start | bytes 983048 | tf_op jit(solution)/shard_map/ppermute | solution.py:271
  107.3 10.3 %collective-permute-start.4 = (f32[80,1024]{1,0:T(8,128)S(1)}, f32[80,1024]{1,0:T(8,128)S(1)}, u32[]{:S(2)}, u32[]{:S(2)}) collective-permute-start(f32[80,1024]{1,0:T(8,128)S(1)} %add.69), channel_id=1, source_target_pairs={{0,1},{1,2},{2,3},{3,0},{4,5},{5,6},{6,7},{7,4},{8,9},{9,10},{10,1... | collective-permute-start | bytes 983048 | tf_op jit(solution)/shard_map/ppermute | solution.py:271

commit v2 on v1

--- a/solution.py
+++ b/solution.py
@@ -10,9 +10,12 @@
 
 
 LOW = 64
+DEPTHS = 8
+REPS = 4
 CHUNK = 256
 TOGETHER = 2
 GRANT = 20 * 1024 * 1024
+SMALL = 8 * 1024 * 1024
 LANES = 128
 BF = jnp.bfloat16
 F32 = jnp.float32
@@ -24,6 +27,87 @@
 def two_parts(x):
     high = lax.reduce_precision(x, exponent_bits=8, mantissa_bits=7)
     return high.astype(BF), (x - high).astype(BF)
+
+
+def split_blocks(blocks):
+    shape = jax.ShapeDtypeStruct(blocks.shape, BF)
+
+    def kernel(x_ref, upper_ref, lower_ref):
+        x = x_ref[...]
+        high = x.astype(BF)
+        upper_ref[...] = high
+        lower_ref[...] = (x - high.astype(F32)).astype(BF)
+
+    part = pl.BlockSpec((4, *blocks.shape[1:]), lambda i: (i, 0, 0))
+    return pl.pallas_call(
+        kernel,
+        grid=(blocks.shape[0] // 4,),
+        in_specs=[part],
+        out_specs=[part, part],
+        out_shape=[shape, shape],
+        compiler_params=pltpu.CompilerParams(vmem_limit_bytes=SMALL),
+        name="split_blocks",
+    )(blocks)
+
+
+def add_blocks(x, y):
+    def kernel(x_ref, y_ref, out_ref):
+        out_ref[...] = x_ref[...] + y_ref[...]
+
+    part = pl.BlockSpec((4, *x.shape[1:]), lambda i: (i, 0, 0))
+    return pl.pallas_call(
+        kernel,
+        grid=(x.shape[0] // 4,),
+        in_specs=[part, part],
+        out_specs=part,
+        out_shape=jax.ShapeDtypeStruct(x.shape, F32),
+        compiler_params=pltpu.CompilerParams(vmem_limit_bytes=SMALL),
+        name="add_blocks",
+    )(x, y)
+
+
+def finish_pool(sums, lengths_t):
+    features, chips, width, lanes = sums.shape
+
+    def kernel(x_ref, lengths_ref, out_ref):
+        share = 1.0 / lengths_ref[pl.ds(pl.program_id(0), 1), :].astype(F32)
+        total = x_ref[0]
+        for chip in range(1, chips):
+            total = total + x_ref[chip]
+        out_ref[...] = total * share
+
+    return pl.pallas_call(
+        kernel,
+        grid=(features,),
+        in_specs=[
+            pl.BlockSpec((None, chips, width, lanes), lambda i: (i, 0, 0, 0)),
+            pl.BlockSpec((features, lanes), lambda i: (0, 0)),
+        ],
+        out_specs=pl.BlockSpec((None, width, lanes), lambda i: (i, 0, 0)),
+        out_shape=jax.ShapeDtypeStruct((features, width, lanes), F32),
+        compiler_params=pltpu.CompilerParams(vmem_limit_bytes=SMALL),
+        name="finish_pool",
+    )(sums, lengths_t)
+
+
+def add_into(block, piece, at):
+    def kernel(block_ref, piece_ref, out_ref):
+        size = piece_ref.shape[0]
+        other = size if at == 0 else 0
+        out_ref[at : at + size] = block_ref[at : at + size] + piece_ref[...]
+        out_ref[other : other + size] = block_ref[other : other + size]
+
+    cols = block.shape[1] // 2
+    spec = lambda x: pl.BlockSpec((x.shape[0], cols), lambda i: (0, i))
+    return pl.pallas_call(
+        kernel,
+        grid=(2,),
+        in_specs=[spec(block), spec(piece)],
+        out_specs=spec(block),
+        out_shape=jax.ShapeDtypeStruct(block.shape, F32),
+        compiler_params=pltpu.CompilerParams(vmem_limit_bytes=SMALL),
+        name="add_into",
+    )(block, piece)
 
 
 def estimate(width, rows, columns):
@@ -106,8 +190,8 @@
     return tile
 
 
-def pool_kernel(per_step, base_ref, ids_ref, upper_ref, lower_ref, out_ref, highs_ref, counts_ref, depth_ref,
-                key_low, key_high, key_count):
+def pool_kernel(per_step, base_ref, ids_ref, upper_ref, lower_ref, out_ref, highs_ref, counts_ref, deep_ref,
+                key_low, key_high, key_count, next_highs, next_counts):
     step = pl.program_id(0)
     width = out_ref.shape[1]
     rows_dev = upper_ref.shape[1]
@@ -117,23 +201,31 @@
         for s in range(per_step):
             layers = first_layers(at * per_step + s, key_low, key_high, key_count)
             for depth in range(2):
-                highs_ref[depth, at * per_step + s] = layers[depth][0]
-                counts_ref[depth, at * per_step + s] = layers[depth][1]
+                next_highs[depth, s] = layers[depth][0]
+                next_counts[depth, s] = layers[depth][1]
 
     @pl.when(step == 0)
     def _():
         deepest = make_keys(base_ref[0], rows_dev, ids_ref, key_low, key_high, key_count)
-        depth_ref[0] = jnp.max(deepest)
-
-        @pl.when(depth_ref[0] > 2)
+        deep_ref[0] = 0
+
+        @pl.when(jnp.max(deepest) > 2)
         def _():
             for s in range(sources):
-                depth_ref[1 + s] = jnp.max(deepest[s : s + 1])
+                def note(depth, carry, s=s):
+                    deep_ref[0] += 1
+                    deep_ref[deep_ref[0]] = s * DEPTHS + depth
+                    return carry
+
+                lax.fori_loop(2, jnp.max(deepest[s : s + 1]), note, 0)
 
         build(0)
 
-    layers = [[(highs_ref[depth, step * per_step + s], counts_ref[depth, step * per_step + s])
-               for depth in range(2)] for s in range(per_step)]
+    layers = [[(next_highs[depth, s], next_counts[depth, s]) for depth in range(2)] for s in range(per_step)]
+    for s in range(per_step):
+        for depth in range(2):
+            highs_ref[depth, s] = layers[s][depth][0]
+            counts_ref[depth, s] = layers[s][depth][1]
     both = lambda cols: jnp.concatenate([upper_ref[:, cols], lower_ref[:, cols]], axis=0)
     chunk = CHUNK
     total = jnp.zeros((2 * width, LANES * per_step), F32)
@@ -148,26 +240,26 @@
 
     build(jnp.minimum(step + 1, sources // per_step - 1))
 
-    @pl.when(depth_ref[0] > 2)
-    def _():
-        for s in range(per_step):
-            source = step * per_step + s
-
-            def deeper(depth, carry):
-                extra = deep_layer(source, depth, key_low, key_high, key_count)
-                wide = 512
-
-                def add(block, value):
-                    tile = jnp.concatenate([counts_for(block * (wide // LOW) + h, [extra])
-                                            for h in range(wide // LOW)], axis=0)
-                    return value + jnp.dot(both(pl.ds(pl.multiple_of(block * wide, wide), wide)),
-                                           tile, preferred_element_type=F32)
-
-                more = lax.fori_loop(0, rows_dev // wide, add, jnp.zeros((2 * width, LANES), F32))
-                out_ref[s] += more[0:width] + more[width : 2 * width]
-                return carry
-
-            lax.fori_loop(2, depth_ref[1 + source], deeper, 0)
+    def deeper(entry, carry):
+        source = deep_ref[1 + entry] // DEPTHS
+
+        @pl.when(source // per_step == step)
+        def _():
+            extra = deep_layer(source, deep_ref[1 + entry] % DEPTHS, key_low, key_high, key_count)
+            wide = 512
+
+            def add(block, value):
+                tile = jnp.concatenate([counts_for(block * (wide // LOW) + h, [extra])
+                                        for h in range(wide // LOW)], axis=0)
+                return value + jnp.dot(both(pl.ds(pl.multiple_of(block * wide, wide), wide)),
+                                       tile, preferred_element_type=F32)
+
+            more = lax.fori_loop(0, rows_dev // wide, add, jnp.zeros((2 * width, LANES), F32))
+            out_ref[source % per_step] += more[0:width] + more[width : 2 * width]
+
+        return carry
+
+    lax.fori_loop(0, deep_ref[0], deeper, 0)
 
 
 def pool(base, ids, parts):
@@ -176,35 +268,39 @@
     per_step = 2
     keys = jax.ShapeDtypeStruct((bag, sources, LANES), F32)
     layer = jax.ShapeDtypeStruct((2, sources, LOW, LANES), BF)
+    shown = pl.BlockSpec((2, per_step, LOW, LANES), lambda i: (0, i, 0, 0))
+    staged = pltpu.VMEM((2, per_step, LOW, LANES), BF)
     return pl.pallas_call(
         functools.partial(pool_kernel, per_step),
         grid=(sources // per_step,),
         in_specs=[SCALARS, WHOLE, WHOLE, WHOLE],
-        out_specs=[pl.BlockSpec((per_step, width, LANES), lambda i: (i, 0, 0)), WHOLE, WHOLE, SCALARS, WHOLE, WHOLE, WHOLE],
+        out_specs=[pl.BlockSpec((per_step, width, LANES), lambda i: (i, 0, 0)), shown, shown, SCALARS, WHOLE, WHOLE, WHOLE],
         out_shape=[
             jax.ShapeDtypeStruct((sources, width, LANES), F32),
             layer,
             layer,
-            jax.ShapeDtypeStruct((1 + sources,), I32),
+            jax.ShapeDtypeStruct((1 + sources * DEPTHS,), I32),
             keys,
             keys,
             keys,
         ],
+        scratch_shapes=[staged, staged],
         compiler_params=pltpu.CompilerParams(dimension_semantics=("arbitrary",), vmem_limit_bytes=GRANT),
         cost_estimate=estimate(width, rows_dev, sources * LANES),
         name="pool",
     )(base, ids, *parts)
 
 
-def grad_kernel(blk, steps, first_ref, *refs):
+def grad_kernel(blk, steps, aheads, rep_ref, *refs):
     halves, outs = [refs[0:8], refs[8:16]], refs[16:]
-    half = outs[0].shape[0]
-    width = 2 * half
+    width = halves[0][0].shape[1]
     step = pl.program_id(0)
-    start = first_ref[step // steps] + step % steps * (blk // LOW)
+    groups = len(aheads)
+    ahead = jnp.where(step < steps, aheads[0], aheads[-1])
+    start = ((rep_ref[0] + ahead) & (REPS - 1)) * (steps * blk // LOW) + step % steps * (blk // LOW)
     together = TOGETHER
     total = jnp.zeros((2 * width, blk), F32)
-    for upper_ref, lower_ref, highs_ref, counts_ref, depth_ref, *keys in halves:
+    for upper_ref, lower_ref, highs_ref, counts_ref, deep_ref, *keys in halves:
         for s in range(0, upper_ref.shape[0], together):
             tile = jnp.concatenate(
                 [jnp.concatenate([counts_for(start + h, [(highs_ref[d, s + t], counts_ref[d, s + t]) for d in range(2)])
@@ -216,50 +312,46 @@
                                             (((1,), (1,)), ((), ())), preferred_element_type=F32)
 
     def put(value, more):
-        for group in range(len(outs) // 2):
+        each = len(outs) // groups
+        for group in range(groups):
             @pl.when(step // steps == group)
             def _():
-                for ref, at in ((outs[2 * group], 0), (outs[2 * group + 1], half)):
-                    new = value[at : at + half] + value[width + at : width + at + half]
+                for part in range(each):
+                    ref, at = outs[each * group + part], part * (width // each)
+                    new = value[at : at + width // each] + value[width + at : width + at + width // each]
                     ref[...] = ref[...] + new if more else new
 
     put(total, False)
 
-    for upper_ref, lower_ref, highs_ref, counts_ref, depth_ref, *keys in halves:
-        @pl.when(depth_ref[0] > 2)
-        def _():
-            def visit(s, carry):
-                def deeper(depth, inner):
-                    extra = deep_layer(s, depth, *keys)
-                    tile = jnp.concatenate([counts_for(start + h, [extra]) for h in range(blk // LOW)], axis=0)
-                    lhs = jnp.concatenate([upper_ref[s], lower_ref[s]], axis=0)
-                    more = lax.dot_general(lhs, tile,
-                                           (((1,), (1,)), ((), ())), preferred_element_type=F32)
-                    put(more, True)
-                    return inner
-
-                return lax.fori_loop(2, depth_ref[1 + s], deeper, carry)
-
-            lax.fori_loop(0, upper_ref.shape[0], visit, 0)
-
-
-def grads(firsts, rows, own, other):
+    for upper_ref, lower_ref, highs_ref, counts_ref, deep_ref, *keys in halves:
+        def deeper(entry, carry, upper_ref=upper_ref, lower_ref=lower_ref, deep_ref=deep_ref, keys=keys):
+            s = deep_ref[1 + entry] // DEPTHS
+            extra = deep_layer(s, deep_ref[1 + entry] % DEPTHS, *keys)
+            tile = jnp.concatenate([counts_for(start + h, [extra]) for h in range(blk // LOW)], axis=0)
+            lhs = jnp.concatenate([upper_ref[s], lower_ref[s]], axis=0)
+            put(lax.dot_general(lhs, tile, (((1,), (1,)), ((), ())), preferred_element_type=F32), True)
+            return carry
+
+        lax.fori_loop(0, deep_ref[0], deeper, 0)
+
+
+def grads(rep, aheads, each, rows, own, other):
     sources, width, _ = own[0].shape
     blk = 256
     steps = rows // blk
-    outs = [pl.BlockSpec((width // 2, blk), lambda i, g=g: (0, jnp.clip(i - g * steps, 0, steps - 1)))
-            for g in range(len(firsts)) for _ in range(2)]
-    each = [WHOLE, WHOLE, WHOLE, WHOLE, SCALARS, WHOLE, WHOLE, WHOLE]
-    return pl.pallas_call(
-        functools.partial(grad_kernel, blk, steps),
-        grid=(steps * len(firsts),),
-        in_specs=[SCALARS] + each + each,
+    outs = [pl.BlockSpec((width // each, blk), lambda i, g=g: (0, jnp.clip(i - g * steps, 0, steps - 1)))
+            for g in range(len(aheads)) for _ in range(each)]
+    side = [WHOLE, WHOLE, WHOLE, WHOLE, SCALARS, WHOLE, WHOLE, WHOLE]
+    return pl.pallas_call(
+        functools.partial(grad_kernel, blk, steps, aheads),
+        grid=(steps * len(aheads),),
+        in_specs=[SCALARS] + side + side,
         out_specs=outs,
-        out_shape=[jax.ShapeDtypeStruct((width // 2, rows), F32)] * len(outs),
+        out_shape=[jax.ShapeDtypeStruct((width // each, rows), F32)] * len(outs),
         compiler_params=pltpu.CompilerParams(dimension_semantics=("arbitrary",), vmem_limit_bytes=GRANT),
-        cost_estimate=estimate(width, rows * len(firsts), 2 * sources * LANES),
+        cost_estimate=estimate(width, rows * len(aheads), 2 * sources * LANES),
         name="grads",
-    )(jnp.stack(firsts).astype(I32) // LOW, *own, *other)
+    )(rep, *own, *other)
 
 
 def to_all(x, axis):
@@ -294,35 +386,35 @@
     ids_other = lax.dynamic_index_in_dim(ids, 1 - core, 1, keepdims=False)
 
     scaled = jnp.transpose(cotangent, (1, 2, 0)) * share[:, None, :]
-    spread_cot = jnp.repeat(scaled, chips, axis=0)
+    spread_cot = jnp.broadcast_to(scaled[:, None], (features, chips, width, examples))
+    spread_cot = spread_cot.reshape(features * chips, width, examples)
     scaled_own = to_all(spread_cot, ("z", "x"))
     scaled_other = shifted(scaled_own, "core", 1)
 
     sent, *layers_other = pool(base, ids_other, parts)
     sent = shifted(sent, "core", 1)
     kept, *layers_own = pool(base, ids_own, parts)
-    pooled = to_all(kept + sent, ("z", "x")).reshape(features, chips, width, examples)
-    pooled = jnp.sum(pooled, axis=1) * share[:, None, :]
-
-    own = [*two_parts(scaled_own), *layers_own]
-    other = [*two_parts(scaled_other), *layers_other]
+    pooled = to_all(add_blocks(kept, sent), ("z", "x")).reshape(features, chips, width, examples)
+    pooled = finish_pool(pooled, lengths_t)
+
+    own = [*split_blocks(scaled_own), *layers_own]
+    other = [*split_blocks(scaled_other), *layers_other]
     rows = rows_dev // reps
 
-    def blocks(*ahead):
-        return grads([(rep + a) % reps * rows for a in ahead], rows, own, other)
-
-    far_top, far_bottom = blocks(2)
+    def blocks(each, *ahead):
+        return grads(rep.astype(I32).reshape(1), ahead, each, rows, own, other)
+
+    half = width // 2
+    far_top, far_bottom = blocks(2, 2)
     from_left = shifted(far_top, "rep", 1)
     from_right = shifted(far_bottom, "rep", -1)
-    next_top, next_bottom, prev_top, prev_bottom = blocks(1, reps - 1)
-    got_bottom = shifted(next_bottom, "rep", 1)
-    got_top = shifted(prev_top, "rep", -1)
-    got_left_top = shifted(next_top + from_left, "rep", 1)
-    got_right_bottom = shifted(prev_bottom + from_right, "rep", -1)
-    here_top, here_bottom = blocks(0)
-    row_grads = jnp.concatenate(
-        [here_top + got_top + got_left_top, here_bottom + got_bottom + got_right_bottom], axis=0
-    )
+    ahead, behind = blocks(1, 1, reps - 1)
+    ahead = add_into(ahead, from_left, 0)
+    behind = add_into(behind, from_right, half)
+    got_left = shifted(ahead, "rep", 1)
+    got_right = shifted(behind, "rep", -1)
+    (here,) = blocks(1, 0)
+    row_grads = here + got_left + got_right
     return jnp.transpose(pooled, (2, 0, 1)), jnp.transpose(row_grads)
 
 

time: 120 us -> 118 us (0.983)
  other arithmetic: 17 us -> 6.73 us
  local copies, waits for them, and re-layouts: 3.69 us -> 11.3 us
  Pallas kernels: 45.3 us -> 52.4 us
  starting transfers between devices: 25.9 us -> 22.2 us
  waiting for transfers between devices: 26.7 us -> 23 us
    unnamed x26 -> x46, local copies, waits for them, and re-layouts: 1.79 us -> 9.39 us
    add x5 -> x0, other arithmetic: 5.68 us -> none  [the longest x1 2.57 us: inner(): kept + sent]
    pallas_call x3 -> x9, Pallas kernels: 23 us -> 28.5 us  [the longest x3 21.7 us: grads(): pl.pallas_call(functools.partial(grad_kernel, blk, steps, aheads), grid=(...]
    convert_element_type x3 -> x1, other arithmetic: 5.77 us -> 2.06 us  [two_parts(): return (high.astype(BF), (x - high).astype(BF))]
    ppermute x8 -> x6, waiting for transfers between devices: 13.9 us -> 10.7 us  [shifted(): return lax.ppermute(x, axis, [(i, (i + by) % n) for i in range(n)])]
    ppermute x8 -> x6, starting transfers between devices: 8.84 us -> 6.54 us  [shifted(): return lax.ppermute(x, axis, [(i, (i + by) % n) for i in range(n)])]
    pallas_call x2, Pallas kernels: 22.3 us -> 23.9 us  [pool(): pl.pallas_call(functools.partial(pool_kernel, per_step), grid=(sources //...]
    reduce_sum x1 -> x0, other arithmetic: 1.42 us -> none  [inner(): pooled = jnp.sum(pooled, axis=1) * share[:, None, :]]
  transfers between devices with their start and end apart: 11 -> 9, of which waited for: 4 -> 4; matrix products, arithmetic and copies ran while one was open for 12% -> 3% of each run, Pallas kernels for 38% -> 45%
where the time goes in v2:
time: 118 us; the launch traced here: 117 us
  Pallas kernels  52.4 us (44%)
  waiting for transfers between devices  23 us (19%)
  starting transfers between devices  22.2 us (19%)
  local copies, waits for them, and re-layouts  11.3 us (10%)
  other arithmetic  6.73 us (6%)
    pallas_call x2, Pallas kernels, pool(): pl.pallas_call(functools.partial(pool_kernel, per_step), grid=(sources //...  23.9 us
    pallas_call x3, Pallas kernels, grads(): pl.pallas_call(functools.partial(grad_kernel, blk, steps, aheads), grid=(...  21.7 us
    all_to_all x3, starting transfers between devices, to_all(): return lax.all_to_all(x, axis, split_axis=0, concat_axis=0, tiled=True)  15.7 us
    all_to_all x3, waiting for transfers between devices, to_all(): return lax.all_to_all(x, axis, split_axis=0, concat_axis=0, tiled=True)  12.2 us
    ppermute x6, waiting for transfers between devices, shifted(): return lax.ppermute(x, axis, [(i, (i + by) % n) for i in range(n)])  10.7 us
    unnamed x46, local copies, waits for them, and re-layouts  9.39 us
    ppermute x6, starting transfers between devices, shifted(): return lax.ppermute(x, axis, [(i, (i + by) % n) for i in range(n)])  6.54 us
    pallas_call x2, Pallas kernels, split_blocks(): pl.pallas_call(kernel, grid=(blocks.shape[0] // 4,), in_specs=[part], out...  2.5 us
  transfers between devices with their start and end apart: 9, of which 4 were waited for; matrix products, arithmetic and copies ran while one was open for 3% of the time, Pallas kernels for 45%

profile of v2, /device:TPU:0, one launch (start us, length us, event | category | flops | bytes accessed | tf_op | source)
XLA Modules:
  0.0 116.5 jit_solution(17079044742409347460)
XLA Ops:
  2.0 8.3 %all-to-all-start = ((s32[32,8,128]{2,1,0:T(8,128)}), s32[32,8,128]{2,1,0:T(8,128)S(1)}, u32[]{:S(2)}, u32[]{:S(2)}) async-start(s32[32,8,128]{2,1,0:T(8,128)} %bitcast.3), calls=%async_computation | async-start | bytes 262144 | tf_op jit(solution)/shard_map/all_to_all | solution.py:358
  12.0 6.1 %all-to-all-done = s32[32,8,128]{2,1,0:T(8,128)S(1)} async-done(((s32[32,8,128]{2,1,0:T(8,128)}), s32[32,8,128]{2,1,0:T(8,128)S(1)}, u32[]{:S(2)}, u32[]{:S(2)}) %all-to-all-start) | async-done | bytes 131104 | tf_op jit(solution)/shard_map/all_to_all | solution.py:358
  18.1 1.2 %broadcast_in_dim.17 = f32[4,4,160,128]{3,2,1,0:T(8,128)} broadcast(f32[4,160,128]{2,1,0:T(8,128)S(1)} %bitcast_multiply_fusion), dimensions={0,2,3} | broadcast | bytes 1638400 | tf_op jit(solution)/shard_map/broadcast_in_dim | solution.py:389
  19.3 3.7 %all-to-all-start.2 = ((f32[16,160,128]{2,1,0:T(8,128)}), f32[16,160,128]{2,1,0:T(8,128)S(1)}, u32[]{:S(2)}, u32[]{:S(2)}) async-start(f32[16,160,128]{2,1,0:T(8,128)} %bitcast.12), calls=%async_computation.2 | async-start | bytes 2621440 | tf_op jit(solution)/shard_map/all_to_all | solution.py:358
  23.0 2.1 %fusion = (bf16[160,4096]{1,0:T(8,128)(2,1)S(1)}, bf16[160,4096]{1,0:T(8,128)(2,1)S(1)}) fusion(f32[4096,160]{0,1:T(8,128)} %param.4), kind=kLoop, calls=%fused_computation.2 | loop fusion | flops 2621440 | bytes 5242880 | tf_op jit(solution)/shard_map/convert_element_type | solution.py:29
  25.1 12.0 %pool.3 = (f32[16,160,128]{2,1,0:T(8,128)}, bf16[2,16,64,128]{3,2,1,0:T(8,128)(2,1)S(1)}, bf16[2,16,64,128]{3,2,1,0:T(8,128)(2,1)S(1)}, s32[129]{0:T(256)S(1)}, ...) custom-call(s32[1]{0:T(128)} %bitcast.base_ref, ...), custom_call_target="tpu_custom_call" | custom-call | flops 5368709120 | bytes 10737418 | tf_op jit(solution)/shard_map/pool/pallas_call | solution.py:273
  38.8 6.2 %all-to-all-done.2.x_ref = f32[16,160,128]{2,1,0:T(8,128)S(1)} async-done(((f32[16,160,128]{2,1,0:T(8,128)}), f32[16,160,128]{2,1,0:T(8,128)S(1)}, u32[]{:S(2)}, u32[]{:S(2)}) %all-to-all-start.2) | async-done | bytes 1310752 | tf_op jit(solution)/shard_map/all_to_all | solution.py:358
  45.0 1.3 %copy-done.2 = bf16[160,4096]{1,0:T(8,128)(2,1)S(1)} copy-done((bf16[160,4096]{1,0:T(8,128)(2,1)S(1)}, bf16[160,4096]{1,0:T(8,128)(2,1)}, u32[]{:S(2)}) %copy-start.2) | copy-done | bytes 1310744
  46.3 11.9 %pool.2 = (f32[16,160,128]{2,1,0:T(8,128)S(1)}, bf16[2,16,64,128]{3,2,1,0:T(8,128)(2,1)S(1)}, bf16[2,16,64,128]{3,2,1,0:T(8,128)(2,1)S(1)}, s32[129]{0:T(256)S(1...) custom-call(s32[1]{0:T(128)} %bitcast.base_ref, ...), custom_call_target="tpu_custom_call" | custom-call | flops 5368709120 | bytes 10737418 | tf_op jit(solution)/shard_map/pool/pallas_call | solution.py:273
  60.6 2.4 %add_blocks.1 = f32[16,160,128]{2,1,0:T(8,128)S(1)} custom-call(f32[16,160,128]{2,1,0:T(8,128)S(1)} %get-tuple-element.24.x_ref, f32[16,160,128]{2,1,0:T(8,128)} %collective-permute-done.y_ref), custom_call_target="tpu_custom_call" | custom-call | tf_op jit(solution)/shard_map/add_blocks/pallas_call | solution.py:58
  63.1 1.1 copy-done
  64.2 3.7 %all-to-all-start.1 = ((f32[16,160,128]{2,1,0:T(8,128)}), f32[16,160,128]{2,1,0:T(8,128)S(1)}, u32[]{:S(2)}, u32[]{:S(2)}) async-start(f32[16,160,128]{2,1,0:T(8,128)} %copy-done), calls=%async_computation.1 | async-start | bytes 2621440 | tf_op jit(solution)/shard_map/all_to_all | solution.py:358
  67.9 2.3 %split_blocks.3 = (bf16[16,160,128]{2,1,0:T(8,128)(2,1)S(1)}, bf16[16,160,128]{2,1,0:T(8,128)(2,1)S(1)}) custom-call(f32[16,160,128]{2,1,0:T(8,128)} %collective-permute-done.1.x_ref), custom_call_target="tpu_custom_call" | custom-call | tf_op jit(solution)/shard_map/split_blocks/pallas_call | solution.py:42
  71.3 1.0 copy-done.14
  72.3 1.0 copy-done.17
  73.4 5.6 %grads.5 = (f32[80,1024]{1,0:T(8,128)S(1)}, f32[80,1024]{1,0:T(8,128)S(1)}) custom-call(s32[1]{0:T(128)} %bitcast.10.rep_ref, bf16[16,160,128]{2,1,0:T(8,128)(2,1)S(1)} %get-tuple-element.26.refs_0_, bf16[16,160,128]{2,1,0:T(8,128)(2,1)S(1)} %copy-done.7, bf16[2,16,64,128]{3,2,1,0:T(8,128)(2,1)S(1)} %copy-done.14, bf16[2,16,64,128]{3,2,1,0:T(8,128)(2,1)S(1)} %copy-done.17, ...), custom_call_target="tpu_custom_call" | custom-call | flops 2684354560 | bytes 5368709 | tf_op jit(solution)/shard_map/grads/pallas_call | solution.py:345
  79.0 3.1 %collective-permute-start.4 = (f32[80,1024]{1,0:T(8,128)S(1)}, f32[80,1024]{1,0:T(8,128)S(1)}, u32[]{:S(2)}, u32[]{:S(2)}) collective-permute-start(f32[80,1024]{1,0:T(8,128)S(1)} %get-tuple-element.45), channel_id=1, source_target_pairs={{0,3},{1,0},{2,1},{3,2},{4,7},{5,4},{6,5},{7,6},{8,11},{9,8},{10,9... | collective-permute-start | bytes 983048 | tf_op jit(solution)/shard_map/ppermute | solution.py:363
  82.1 10.7 %grads.4 = (f32[160,1024]{1,0:T(8,128)S(1)}, f32[160,1024]{1,0:T(8,128)S(1)}) custom-call(s32[1]{0:T(128)} %bitcast.10.rep_ref, bf16[16,160,128]{2,1,0:T(8,128)(2,1)S(1)} %get-tuple-element.26.refs_0_, bf16[16,160,128]{2,1,0:T(8,128)(2,1)S(1)} %copy-done.7, bf16[2,16,64,128]{3,2,1,0:T(8,128)(2,1)S(1)} %copy-done.15, bf16[2,16,64,128]{3,2,1,0:T(8,128)(2,1)S(1)} %copy-done.18, ...), custom_call_target="tpu_custom_call" | custom-call | flops 5368709120 | bytes 10737418 | tf_op jit(solution)/shard_map/grads/pallas_call | solution.py:345
  93.0 3.3 %collective-permute-start.5 = (f32[160,1024]{1,0:T(8,128)S(1)}, f32[160,1024]{1,0:T(8,128)}, u32[]{:S(2)}, u32[]{:S(2)}) collective-permute-start(f32[160,1024]{1,0:T(8,128)S(1)} %add_into.3), channel_id=1, source_target_pairs={{0,3},{1,0},{2,1},{3,2},{4,7},{5,4},{6,5},{7,6},{8,11},{9,8},{10,9... | collective-permute-start | bytes 1966088 | tf_op jit(solution)/shard_map/ppermute | solution.py:363
  96.7 5.5 %grads.3 = f32[160,1024]{1,0:T(8,128)S(1)} custom-call(s32[1]{0:T(128)} %bitcast.10.rep_ref, bf16[16,160,128]{2,1,0:T(8,128)(2,1)S(1)} %copy-done.5, bf16[16,160,128]{2,1,0:T(8,128)(2,1)S(1)} %copy-done.7, bf16[2,16,64,128]{3,2,1,0:T(8,128)(2,1)S(1)} %copy-done.15, bf16[2,16,64,128]{3,2,1,0:T(8,128)(2,1)S(1)} %copy-done.18, ...), custom_call_target="tpu_custom_call" | custom-call | flops 2684354560 | bytes 5368709 | tf_op jit(solution)/shard_map/grads/pallas_call | solution.py:345
  102.2 1.4 %finish_pool.1 = f32[4,160,128]{2,1,0:T(8,128)} custom-call(f32[4,4,160,128]{3,2,1,0:T(8,128)S(1)} %bitcast.22, s32[4,128]{1,0:T(4,128)S(1)} %bitcast.24), custom_call_target="tpu_custom_call" | custom-call | tf_op jit(solution)/shard_map/finish_pool/pallas_call | solution.py:79
  103.6 6.9 %collective-permute-done.5 = f32[160,1024]{1,0:T(8,128)} collective-permute-done((f32[160,1024]{1,0:T(8,128)S(1)}, f32[160,1024]{1,0:T(8,128)}, u32[]{:S(2)}, u32[]{:S(2)}) %collective-permute-start.5) | collective-permute-done | bytes 655392 | tf_op jit(solution)/shard_map/ppermute | solution.py:363
  110.4 3.8 %collective-permute-done.3 = f32[160,1024]{1,0:T(8,128)} collective-permute-done((f32[160,1024]{1,0:T(8,128)S(1)}, f32[160,1024]{1,0:T(8,128)}, u32[]{:S(2)}, u32[]{:S(2)}) %collective-permute-start.3) | collective-permute-done | bytes 655392 | tf_op jit(solution)/shard_map/ppermute | solution.py:363
  114.3 2.3 %add_bitcast_fusion = f32[1024,160]{0,1:T(8,128)} fusion(f32[160,1024]{1,0:T(8,128)} %collective-permute-done.5, f32[160,1024]{1,0:T(8,128)S(1)} %grads.3, f32[160,1024]{1,0:T(8,128)} %collective-permute-done.3), kind=kLoop, calls=%fused_computation.3 | loop fusion | flops 327680 | bytes 2621440 | tf_op jit(solution)/shard_map/transpose | solution.py:418
  (59 shorter events, 8.9 us)
Async XLA Ops:
  2.0 16.1 %all-to-all-start = ((s32[32,8,128]{2,1,0:T(8,128)}), s32[32,8,128]{2,1,0:T(8,128)S(1)}, u32[]{:S(2)}, u32[]{:S(2)}) async-start(s32[32,8,128]{2,1,0:T(8,128)} %bitcast.3), calls=%async_computation | async-start | bytes 262144 | tf_op jit(solution)/shard_map/all_to_all | solution.py:358
  19.3 25.7 %all-to-all-start.2 = ((f32[16,160,128]{2,1,0:T(8,128)}), f32[16,160,128]{2,1,0:T(8,128)S(1)}, u32[]{:S(2)}, u32[]{:S(2)}) async-start(f32[16,160,128]{2,1,0:T(8,128)} %bitcast.12), calls=%async_computation.2 | async-start | bytes 2621440 | tf_op jit(solution)/shard_map/all_to_all | solution.py:358
  25.0 12.1 %copy-start.1 = (bf16[160,4096]{1,0:T(8,128)(2,1)}, bf16[160,4096]{1,0:T(8,128)(2,1)S(1)}, u32[]{:S(2)}) copy-start(bf16[160,4096]{1,0:T(8,128)(2,1)S(1)} %get-tuple-element.47.upper_ref) | copy-start | bytes 3932164
  38.7 21.9 %collective-permute-start = (f32[16,160,128]{2,1,0:T(8,128)}, f32[16,160,128]{2,1,0:T(8,128)}, u32[]{:S(2)}, u32[]{:S(2)}) collective-permute-start(f32[16,160,128]{2,1,0:T(8,128)} %get-tuple-element.25), channel_id=1, source_target_pairs={{0,4},{4,0},{1,5},{5,1},{2,6},{6,2},{3,7},{7,3},{8,12},{12,8},{9,1... | collective-permute-start | bytes 3932168 | tf_op jit(solution)/shard_map/ppermute | solution.py:363
  45.0 22.9 %collective-permute-start.1 = (f32[16,160,128]{2,1,0:T(8,128)S(1)}, f32[16,160,128]{2,1,0:T(8,128)}, u32[]{:S(2)}, u32[]{:S(2)}) collective-permute-start(f32[16,160,128]{2,1,0:T(8,128)S(1)} %all-to-all-done.2.x_ref), channel_id=1, source_target_pairs={{0,4},{4,0},{1,5},{5,1},{2,6},{6,2},{3,7},{7,3},{8,12},{12,8},{9,1... | collective-permute-start | bytes 3932168 | tf_op jit(solution)/shard_map/ppermute | solution.py:363
  45.0 1.3 %copy-start.2 = (bf16[160,4096]{1,0:T(8,128)(2,1)S(1)}, bf16[160,4096]{1,0:T(8,128)(2,1)}, u32[]{:S(2)}) copy-start(bf16[160,4096]{1,0:T(8,128)(2,1)} %copy-done.1) | copy-start | bytes 3932164
  59.5 1.2 %copy-start.13 = (bf16[2,16,64,128]{3,2,1,0:T(8,128)(2,1)}, bf16[2,16,64,128]{3,2,1,0:T(8,128)(2,1)S(1)}, u32[]{:S(2)}) copy-start(bf16[2,16,64,128]{3,2,1,0:T(8,128)(2,1)S(1)} %get-tuple-element.28.refs_2_) | copy-start | bytes 1572868
  59.5 1.2 %copy-start.16 = (bf16[2,16,64,128]{3,2,1,0:T(8,128)(2,1)}, bf16[2,16,64,128]{3,2,1,0:T(8,128)(2,1)S(1)}, u32[]{:S(2)}) copy-start(bf16[2,16,64,128]{3,2,1,0:T(8,128)(2,1)S(1)} %get-tuple-element.29.refs_3_) | copy-start | bytes 1572868
  60.6 21.4 %copy-start.4 = (bf16[16,160,128]{2,1,0:T(8,128)(2,1)}, bf16[16,160,128]{2,1,0:T(8,128)(2,1)S(1)}, u32[]{:S(2)}) copy-start(bf16[16,160,128]{2,1,0:T(8,128)(2,1)S(1)} %get-tuple-element.26.refs_0_) | copy-start | bytes 1966084
  63.1 1.1 copy-start
  64.2 38.0 %all-to-all-start.1 = ((f32[16,160,128]{2,1,0:T(8,128)}), f32[16,160,128]{2,1,0:T(8,128)S(1)}, u32[]{:S(2)}, u32[]{:S(2)}) async-start(f32[16,160,128]{2,1,0:T(8,128)} %copy-done), calls=%async_computation.1 | async-start | bytes 2621440 | tf_op jit(solution)/shard_map/all_to_all | solution.py:358
  67.9 2.3 %copy-start.7 = (bf16[16,160,128]{2,1,0:T(8,128)(2,1)S(1)}, bf16[16,160,128]{2,1,0:T(8,128)(2,1)}, u32[]{:S(2)}) copy-start(bf16[16,160,128]{2,1,0:T(8,128)(2,1)} %copy-done.6) | copy-start | bytes 1966084
  67.9 2.3 %copy-start.9 = (bf16[2,16,64,128]{3,2,1,0:T(8,128)(2,1)S(1)}, bf16[2,16,64,128]{3,2,1,0:T(8,128)(2,1)}, u32[]{:S(2)}) copy-start(bf16[2,16,64,128]{3,2,1,0:T(8,128)(2,1)} %copy-done.8) | copy-start | bytes 1572868
  67.9 2.3 %copy-start.20 = (f32[8,16,128]{2,1,0:T(8,128)S(1)}, f32[8,16,128]{2,1,0:T(8,128)}, u32[]{:S(2)}) copy-start(f32[8,16,128]{2,1,0:T(8,128)} %copy-done.19) | copy-start | bytes 196612
  67.9 2.3 %copy-start.22 = (f32[8,16,128]{2,1,0:T(8,128)S(1)}, f32[8,16,128]{2,1,0:T(8,128)}, u32[]{:S(2)}) copy-start(f32[8,16,128]{2,1,0:T(8,128)} %copy-done.21) | copy-start | bytes 196612
  73.4 8.7 %copy-start.15 = (bf16[2,16,64,128]{3,2,1,0:T(8,128)(2,1)S(1)}, bf16[2,16,64,128]{3,2,1,0:T(8,128)(2,1)}, u32[]{:S(2)}) copy-start(bf16[2,16,64,128]{3,2,1,0:T(8,128)(2,1)} %copy-done.13) | copy-start | bytes 1572868
  73.4 8.7 %copy-start.18 = (bf16[2,16,64,128]{3,2,1,0:T(8,128)(2,1)S(1)}, bf16[2,16,64,128]{3,2,1,0:T(8,128)(2,1)}, u32[]{:S(2)}) copy-start(bf16[2,16,64,128]{3,2,1,0:T(8,128)(2,1)} %copy-done.16) | copy-start | bytes 1572868
  79.0 13.8 %collective-permute-start.4 = (f32[80,1024]{1,0:T(8,128)S(1)}, f32[80,1024]{1,0:T(8,128)S(1)}, u32[]{:S(2)}, u32[]{:S(2)}) collective-permute-start(f32[80,1024]{1,0:T(8,128)S(1)} %get-tuple-element.45), channel_id=1, source_target_pairs={{0,3},{1,0},{2,1},{3,2},{4,7},{5,4},{6,5},{7,6},{8,11},{9,8},{10,9... | collective-permute-start | bytes 983048 | tf_op jit(solution)/shard_map/ppermute | solution.py:363
  82.0 14.3 %collective-permute-start.2 = (f32[80,1024]{1,0:T(8,128)S(1)}, f32[80,1024]{1,0:T(8,128)S(1)}, u32[]{:S(2)}, u32[]{:S(2)}) collective-permute-start(f32[80,1024]{1,0:T(8,128)S(1)} %get-tuple-element.43), channel_id=1, source_target_pairs={{0,1},{1,2},{2,3},{3,0},{4,5},{5,6},{6,7},{7,4},{8,9},{9,10},{10,1... | collective-permute-start | bytes 983048 | tf_op jit(solution)/shard_map/ppermute | solution.py:363
  92.8 3.9 %copy-start.5 = (bf16[16,160,128]{2,1,0:T(8,128)(2,1)S(1)}, bf16[16,160,128]{2,1,0:T(8,128)(2,1)}, u32[]{:S(2)}) copy-start(bf16[16,160,128]{2,1,0:T(8,128)(2,1)} %copy-done.4) | copy-start | bytes 1966084
  92.8 3.9 %copy-start.12 = (bf16[2,16,64,128]{3,2,1,0:T(8,128)(2,1)S(1)}, bf16[2,16,64,128]{3,2,1,0:T(8,128)(2,1)}, u32[]{:S(2)}) copy-start(bf16[2,16,64,128]{3,2,1,0:T(8,128)(2,1)} %copy-done.10) | copy-start | bytes 1572868
  93.0 17.4 %collective-permute-start.5 = (f32[160,1024]{1,0:T(8,128)S(1)}, f32[160,1024]{1,0:T(8,128)}, u32[]{:S(2)}, u32[]{:S(2)}) collective-permute-start(f32[160,1024]{1,0:T(8,128)S(1)} %add_into.3), channel_id=1, source_target_pairs={{0,3},{1,0},{2,1},{3,2},{4,7},{5,4},{6,5},{7,6},{8,11},{9,8},{10,9... | collective-permute-start | bytes 1966088 | tf_op jit(solution)/shard_map/ppermute | solution.py:363
  96.6 5.6 %copy-start.3 = (s32[128,4]{0,1:T(4,128)S(1)}, s32[128,4]{0,1:T(4,128)}, u32[]{:S(2)}) copy-start(s32[128,4]{0,1:T(4,128)} %param.6) | copy-start | bytes 6148
  96.6 17.7 %collective-permute-start.3 = (f32[160,1024]{1,0:T(8,128)S(1)}, f32[160,1024]{1,0:T(8,128)}, u32[]{:S(2)}, u32[]{:S(2)}) collective-permute-start(f32[160,1024]{1,0:T(8,128)S(1)} %add_into.2), channel_id=1, source_target_pairs={{0,1},{1,2},{2,3},{3,0},{4,5},{5,6},{6,7},{7,4},{8,9},{9,10},{10,1... | collective-permute-start | bytes 1966088 | tf_op jit(solution)/shard_map/ppermute | solution.py:363
  (8 other events, 6.9 us)

commit v3 on v2

--- a/solution.py
+++ b/solution.py
@@ -12,10 +12,10 @@
 LOW = 64
 DEPTHS = 8
 REPS = 4
+SMALL = 8 * 1024 * 1024
 CHUNK = 256
 TOGETHER = 2
 GRANT = 20 * 1024 * 1024
-SMALL = 8 * 1024 * 1024
 LANES = 128
 BF = jnp.bfloat16
 F32 = jnp.float32
@@ -27,43 +27,6 @@
 def two_parts(x):
     high = lax.reduce_precision(x, exponent_bits=8, mantissa_bits=7)
     return high.astype(BF), (x - high).astype(BF)
-
-
-def split_blocks(blocks):
-    shape = jax.ShapeDtypeStruct(blocks.shape, BF)
-
-    def kernel(x_ref, upper_ref, lower_ref):
-        x = x_ref[...]
-        high = x.astype(BF)
-        upper_ref[...] = high
-        lower_ref[...] = (x - high.astype(F32)).astype(BF)
-
-    part = pl.BlockSpec((4, *blocks.shape[1:]), lambda i: (i, 0, 0))
-    return pl.pallas_call(
-        kernel,
-        grid=(blocks.shape[0] // 4,),
-        in_specs=[part],
-        out_specs=[part, part],
-        out_shape=[shape, shape],
-        compiler_params=pltpu.CompilerParams(vmem_limit_bytes=SMALL),
-        name="split_blocks",
-    )(blocks)
-
-
-def add_blocks(x, y):
-    def kernel(x_ref, y_ref, out_ref):
-        out_ref[...] = x_ref[...] + y_ref[...]
-
-    part = pl.BlockSpec((4, *x.shape[1:]), lambda i: (i, 0, 0))
-    return pl.pallas_call(
-        kernel,
-        grid=(x.shape[0] // 4,),
-        in_specs=[part, part],
-        out_specs=part,
-        out_shape=jax.ShapeDtypeStruct(x.shape, F32),
-        compiler_params=pltpu.CompilerParams(vmem_limit_bytes=SMALL),
-        name="add_blocks",
-    )(x, y)
 
 
 def finish_pool(sums, lengths_t):
@@ -90,24 +53,25 @@
     )(sums, lengths_t)
 
 
-def add_into(block, piece, at):
-    def kernel(block_ref, piece_ref, out_ref):
-        size = piece_ref.shape[0]
-        other = size if at == 0 else 0
-        out_ref[at : at + size] = block_ref[at : at + size] + piece_ref[...]
-        out_ref[other : other + size] = block_ref[other : other + size]
-
-    cols = block.shape[1] // 2
-    spec = lambda x: pl.BlockSpec((x.shape[0], cols), lambda i: (0, i))
+def join(tops, bottoms):
+    half, rows = tops[0].shape
+    cols = rows // 2
+
+    def kernel(*refs):
+        out_ref = refs[-1]
+        out_ref[0:half] = refs[0][...] + refs[1][...] + refs[2][...]
+        out_ref[half:] = refs[3][...] + refs[4][...] + refs[5][...]
+
+    spec = lambda n: pl.BlockSpec((n, cols), lambda i: (0, i))
     return pl.pallas_call(
         kernel,
         grid=(2,),
-        in_specs=[spec(block), spec(piece)],
-        out_specs=spec(block),
-        out_shape=jax.ShapeDtypeStruct(block.shape, F32),
+        in_specs=[spec(half)] * 6,
+        out_specs=spec(2 * half),
+        out_shape=jax.ShapeDtypeStruct((2 * half, rows), F32),
         compiler_params=pltpu.CompilerParams(vmem_limit_bytes=SMALL),
-        name="add_into",
-    )(block, piece)
+        name="join",
+    )(*tops, *bottoms)
 
 
 def estimate(width, rows, columns):
@@ -191,7 +155,7 @@
 
 
 def pool_kernel(per_step, base_ref, ids_ref, upper_ref, lower_ref, out_ref, highs_ref, counts_ref, deep_ref,
-                key_low, key_high, key_count, next_highs, next_counts):
+                key_low, key_high, key_count):
     step = pl.program_id(0)
     width = out_ref.shape[1]
     rows_dev = upper_ref.shape[1]
@@ -201,8 +165,8 @@
         for s in range(per_step):
             layers = first_layers(at * per_step + s, key_low, key_high, key_count)
             for depth in range(2):
-                next_highs[depth, s] = layers[depth][0]
-                next_counts[depth, s] = layers[depth][1]
+                highs_ref[depth, at * per_step + s] = layers[depth][0]
+                counts_ref[depth, at * per_step + s] = layers[depth][1]
 
     @pl.when(step == 0)
     def _():
@@ -221,11 +185,8 @@
 
         build(0)
 
-    layers = [[(next_highs[depth, s], next_counts[depth, s]) for depth in range(2)] for s in range(per_step)]
-    for s in range(per_step):
-        for depth in range(2):
-            highs_ref[depth, s] = layers[s][depth][0]
-            counts_ref[depth, s] = layers[s][depth][1]
+    layers = [[(highs_ref[depth, step * per_step + s], counts_ref[depth, step * per_step + s])
+               for depth in range(2)] for s in range(per_step)]
     both = lambda cols: jnp.concatenate([upper_ref[:, cols], lower_ref[:, cols]], axis=0)
     chunk = CHUNK
     total = jnp.zeros((2 * width, LANES * per_step), F32)
@@ -268,13 +229,11 @@
     per_step = 2
     keys = jax.ShapeDtypeStruct((bag, sources, LANES), F32)
     layer = jax.ShapeDtypeStruct((2, sources, LOW, LANES), BF)
-    shown = pl.BlockSpec((2, per_step, LOW, LANES), lambda i: (0, i, 0, 0))
-    staged = pltpu.VMEM((2, per_step, LOW, LANES), BF)
     return pl.pallas_call(
         functools.partial(pool_kernel, per_step),
         grid=(sources // per_step,),
         in_specs=[SCALARS, WHOLE, WHOLE, WHOLE],
-        out_specs=[pl.BlockSpec((per_step, width, LANES), lambda i: (i, 0, 0)), shown, shown, SCALARS, WHOLE, WHOLE, WHOLE],
+        out_specs=[pl.BlockSpec((per_step, width, LANES), lambda i: (i, 0, 0)), WHOLE, WHOLE, SCALARS, WHOLE, WHOLE, WHOLE],
         out_shape=[
             jax.ShapeDtypeStruct((sources, width, LANES), F32),
             layer,
@@ -284,7 +243,6 @@
             keys,
             keys,
         ],
-        scratch_shapes=[staged, staged],
         compiler_params=pltpu.CompilerParams(dimension_semantics=("arbitrary",), vmem_limit_bytes=GRANT),
         cost_estimate=estimate(width, rows_dev, sources * LANES),
         name="pool",
@@ -394,27 +352,26 @@
     sent, *layers_other = pool(base, ids_other, parts)
     sent = shifted(sent, "core", 1)
     kept, *layers_own = pool(base, ids_own, parts)
-    pooled = to_all(add_blocks(kept, sent), ("z", "x")).reshape(features, chips, width, examples)
+    pooled = to_all(kept + sent, ("z", "x")).reshape(features, chips, width, examples)
     pooled = finish_pool(pooled, lengths_t)
 
-    own = [*split_blocks(scaled_own), *layers_own]
-    other = [*split_blocks(scaled_other), *layers_other]
+    own = [*two_parts(scaled_own), *layers_own]
+    other = [*two_parts(scaled_other), *layers_other]
     rows = rows_dev // reps
 
-    def blocks(each, *ahead):
-        return grads(rep.astype(I32).reshape(1), ahead, each, rows, own, other)
-
-    half = width // 2
-    far_top, far_bottom = blocks(2, 2)
+    def blocks(*ahead):
+        return grads(rep.astype(I32).reshape(1), ahead, 2, rows, own, other)
+
+    far_top, far_bottom = blocks(2)
     from_left = shifted(far_top, "rep", 1)
     from_right = shifted(far_bottom, "rep", -1)
-    ahead, behind = blocks(1, 1, reps - 1)
-    ahead = add_into(ahead, from_left, 0)
-    behind = add_into(behind, from_right, half)
-    got_left = shifted(ahead, "rep", 1)
-    got_right = shifted(behind, "rep", -1)
-    (here,) = blocks(1, 0)
-    row_grads = here + got_left + got_right
+    next_top, next_bottom, prev_top, prev_bottom = blocks(1, reps - 1)
+    got_bottom = shifted(next_bottom, "rep", 1)
+    got_top = shifted(prev_top, "rep", -1)
+    got_left_top = shifted(next_top + from_left, "rep", 1)
+    got_right_bottom = shifted(prev_bottom + from_right, "rep", -1)
+    here_top, here_bottom = blocks(0)
+    row_grads = join([here_top, got_top, got_left_top], [here_bottom, got_bottom, got_right_bottom])
     return jnp.transpose(pooled, (2, 0, 1)), jnp.transpose(row_grads)
 
 

time: 118 us -> 111 us (0.941)
  local copies, waits for them, and re-layouts: 11.3 us -> 4.26 us
  other arithmetic: 6.73 us -> 12.2 us
  waiting for transfers between devices: 23 us -> 18.3 us
  Pallas kernels: 52.4 us -> 48.6 us
  starting transfers between devices: 22.2 us -> 25.1 us
    unnamed x46 -> x34, local copies, waits for them, and re-layouts: 9.39 us -> 2.35 us
    ppermute x6 -> x8, waiting for transfers between devices: 10.7 us -> 4.27 us  [shifted(): return lax.ppermute(x, axis, [(i, (i + by) % n) for i in range(n)])]
    add x0 -> x3, other arithmetic: none -> 4.07 us  [the longest x1 2.54 us: inner(): kept + sent]
    convert_element_type x1 -> x3, other arithmetic: 2.06 us -> 5.74 us  [two_parts(): return (high.astype(BF), (x - high).astype(BF))]
    pallas_call x5 -> x1, Pallas kernels: 5.37 us -> 1.99 us  [join(): pl.pallas_call(kernel, grid=(2,), in_specs=[spec(half)] * 6, out_specs=sp...]
    transpose x1 -> x0, other arithmetic: 2.26 us -> none  [inner(): return (jnp.transpose(pooled, (2, 0, 1)), jnp.transpose(row_grads))]
    ppermute x6 -> x8, starting transfers between devices: 6.54 us -> 8.77 us  [shifted(): return lax.ppermute(x, axis, [(i, (i + by) % n) for i in range(n)])]
    pallas_call x2, Pallas kernels: 23.9 us -> 22.1 us  [pool(): pl.pallas_call(functools.partial(pool_kernel, per_step), grid=(sources //...]
  transfers between devices with their start and end apart: 9 -> 11, of which waited for: 4 -> 3; matrix products, arithmetic and copies ran while one was open for 3% -> 11% of each run, Pallas kernels for 45% -> 43%
where the time goes in v3:
time: 111 us; the launch traced here: 109 us
  Pallas kernels  48.6 us (44%)
  starting transfers between devices  25.1 us (23%)
  waiting for transfers between devices  18.3 us (16%)
  other arithmetic  12.2 us (11%)
  local copies, waits for them, and re-layouts  4.26 us (4%)
    pallas_call x3, Pallas kernels, grads(): pl.pallas_call(functools.partial(grad_kernel, blk, steps, aheads), grid=(...  23.1 us
    pallas_call x2, Pallas kernels, pool(): pl.pallas_call(functools.partial(pool_kernel, per_step), grid=(sources //...  22.1 us
    all_to_all x3, starting transfers between devices, to_all(): return lax.all_to_all(x, axis, split_axis=0, concat_axis=0, tiled=True)  16.4 us
    all_to_all x3, waiting for transfers between devices, to_all(): return lax.all_to_all(x, axis, split_axis=0, concat_axis=0, tiled=True)  14 us
    ppermute x8, starting transfers between devices, shifted(): return lax.ppermute(x, axis, [(i, (i + by) % n) for i in range(n)])  8.77 us
    convert_element_type x3, other arithmetic, two_parts(): return (high.astype(BF), (x - high).astype(BF))  5.74 us
    ppermute x8, waiting for transfers between devices, shifted(): return lax.ppermute(x, axis, [(i, (i + by) % n) for i in range(n)])  4.27 us
    add x1, other arithmetic, inner(): kept + sent  2.54 us
  transfers between devices with their start and end apart: 11, of which 3 were waited for; matrix products, arithmetic and copies ran while one was open for 11% of the time, Pallas kernels for 43%

profile of v3, /device:TPU:0, one launch (start us, length us, event | category | flops | bytes accessed | tf_op | source)
XLA Modules:
  0.0 109.3 jit_solution(11214379041359125413)
XLA Ops:
  2.0 8.3 %all-to-all-start = ((s32[32,8,128]{2,1,0:T(8,128)}), s32[32,8,128]{2,1,0:T(8,128)S(1)}, u32[]{:S(2)}, u32[]{:S(2)}) async-start(s32[32,8,128]{2,1,0:T(8,128)} %bitcast.3), calls=%async_computation | async-start | bytes 262144 | tf_op jit(solution)/shard_map/all_to_all | solution.py:316
  11.0 1.0 bitcast_multiply_fusion
  12.0 6.1 %all-to-all-done = s32[32,8,128]{2,1,0:T(8,128)S(1)} async-done(((s32[32,8,128]{2,1,0:T(8,128)}), s32[32,8,128]{2,1,0:T(8,128)S(1)}, u32[]{:S(2)}, u32[]{:S(2)}) %all-to-all-start) | async-done | bytes 131104 | tf_op jit(solution)/shard_map/all_to_all | solution.py:316
  18.1 1.2 %broadcast_in_dim.17 = f32[4,4,160,128]{3,2,1,0:T(8,128)} broadcast(f32[4,160,128]{2,1,0:T(8,128)S(1)} %bitcast_multiply_fusion), dimensions={0,2,3} | broadcast | bytes 1638400 | tf_op jit(solution)/shard_map/broadcast_in_dim | solution.py:347
  19.3 4.4 %all-to-all-start.2 = ((f32[16,160,128]{2,1,0:T(8,128)}), f32[16,160,128]{2,1,0:T(8,128)}, u32[]{:S(2)}, u32[]{:S(2)}) async-start(f32[16,160,128]{2,1,0:T(8,128)} %bitcast.12), calls=%async_computation.2 | async-start | bytes 2621440 | tf_op jit(solution)/shard_map/all_to_all | solution.py:316
  23.7 2.2 %fusion = (bf16[160,4096]{1,0:T(8,128)(2,1)S(1)}, bf16[160,4096]{1,0:T(8,128)(2,1)S(1)}) fusion(f32[4096,160]{0,1:T(8,128)} %param.4), kind=kLoop, calls=%fused_computation.2 | loop fusion | flops 2621440 | bytes 5242880 | tf_op jit(solution)/shard_map/convert_element_type | solution.py:29
  25.9 11.0 %pool.3 = (f32[16,160,128]{2,1,0:T(8,128)}, bf16[2,16,64,128]{3,2,1,0:T(8,128)(2,1)S(1)}, bf16[2,16,64,128]{3,2,1,0:T(8,128)(2,1)S(1)}, s32[129]{0:T(256)S(1)}, ...) custom-call(s32[1]{0:T(128)} %bitcast.base_ref, ...), custom_call_target="tpu_custom_call" | custom-call | flops 5368709120 | bytes 10737418 | tf_op jit(solution)/shard_map/pool/pallas_call | solution.py:232
  36.9 0.8 copy-done.7
  37.8 7.9 %all-to-all-done.2 = f32[16,160,128]{2,1,0:T(8,128)} async-done(((f32[16,160,128]{2,1,0:T(8,128)}), f32[16,160,128]{2,1,0:T(8,128)}, u32[]{:S(2)}, u32[]{:S(2)}) %all-to-all-start.2) | async-done | bytes 1310752 | tf_op jit(solution)/shard_map/all_to_all | solution.py:316
  45.8 11.1 %pool.2 = (f32[16,160,128]{2,1,0:T(8,128)S(1)}, bf16[2,16,64,128]{3,2,1,0:T(8,128)(2,1)S(1)}, bf16[2,16,64,128]{3,2,1,0:T(8,128)(2,1)S(1)}, s32[129]{0:T(256)S(1...) custom-call(s32[1]{0:T(128)} %bitcast.base_ref, ...), custom_call_target="tpu_custom_call" | custom-call | flops 5368709120 | bytes 10737418 | tf_op jit(solution)/shard_map/pool/pallas_call | solution.py:232
  56.9 1.9 %fusion.1 = (bf16[16,160,128]{2,1,0:T(8,128)(2,1)S(1)}, bf16[16,160,128]{2,1,0:T(8,128)(2,1)S(1)}) fusion(f32[16,160,128]{2,1,0:T(8,128)} %all-to-all-done.2), kind=kLoop, calls=%fused_computation.7 | loop fusion | flops 1310720 | bytes 2621440 | tf_op jit(solution)/shard_map/convert_element_type | solution.py:29
  58.9 2.5 %add.23 = f32[16,160,128]{2,1,0:T(8,128)} add(f32[16,160,128]{2,1,0:T(8,128)S(1)} %get-tuple-element.24, f32[16,160,128]{2,1,0:T(8,128)} %collective-permute-done) | non-fusion elementwise | flops 327680 | bytes 3932160 | tf_op jit(solution)/shard_map/add | solution.py:355
  61.5 3.7 %all-to-all-start.1 = ((f32[16,160,128]{2,1,0:T(8,128)}), f32[16,160,128]{2,1,0:T(8,128)S(1)}, u32[]{:S(2)}, u32[]{:S(2)}) async-start(f32[16,160,128]{2,1,0:T(8,128)} %add.23), calls=%async_computation.1 | async-start | bytes 2621440 | tf_op jit(solution)/shard_map/all_to_all | solution.py:316
  65.2 1.6 %fusion.2 = (bf16[16,160,128]{2,1,0:T(8,128)(2,1)S(1)}, bf16[16,160,128]{2,1,0:T(8,128)(2,1)S(1)}) fusion(f32[16,160,128]{2,1,0:T(8,128)} %collective-permute-done.1), kind=kLoop, calls=%fused_computation.8 | loop fusion | flops 1310720 | bytes 2621440 | tf_op jit(solution)/shard_map/convert_element_type | solution.py:29
  66.9 5.7 %grads.5 = (f32[80,1024]{1,0:T(8,128)S(1)}, f32[80,1024]{1,0:T(8,128)S(1)}) custom-call(s32[1]{0:T(128)} %bitcast.10.rep_ref, bf16[16,160,128]{2,1,0:T(8,128)(2,1)S(1)} %get-tuple-element.51.refs_0_, bf16[16,160,128]{2,1,0:T(8,128)(2,1)S(1)} %get-tuple-element.50.refs_1_, bf16[2,16,64,128]{3,2,1,0:T(8,128)(2,1)S(1)} %copy-done.10, ...), custom_call_target="tpu_custom_call" | custom-call | flops 2684354560 | bytes 5368709 | tf_op jit(solution)/shard_map/grads/pallas_call | solution.py:303
  72.7 1.6 %collective-permute-start.3 = (f32[80,1024]{1,0:T(8,128)S(1)}, f32[80,1024]{1,0:T(8,128)S(1)}, u32[]{:S(2)}, u32[]{:S(2)}) collective-permute-start(f32[80,1024]{1,0:T(8,128)S(1)} %get-tuple-element.41), channel_id=1, source_target_pairs={{0,1},{1,2},{2,3},{3,0},{4,5},{5,6},{6,7},{7,4},{8,9},{9,10},{10,1... | collective-permute-start | bytes 983048 | tf_op jit(solution)/shard_map/ppermute | solution.py:321
  74.3 1.7 %collective-permute-start.6 = (f32[80,1024]{1,0:T(8,128)S(1)}, f32[80,1024]{1,0:T(8,128)S(1)}, u32[]{:S(2)}, u32[]{:S(2)}) collective-permute-start(f32[80,1024]{1,0:T(8,128)S(1)} %get-tuple-element.45), channel_id=1, source_target_pairs={{0,3},{1,0},{2,1},{3,2},{4,7},{5,4},{6,5},{7,6},{8,11},{9,8},{10,9... | collective-permute-start | bytes 983048 | tf_op jit(solution)/shard_map/ppermute | solution.py:321
  76.0 11.7 %grads.4 = (f32[80,1024]{1,0:T(8,128)S(1)}, f32[80,1024]{1,0:T(8,128)}, f32[80,1024]{1,0:T(8,128)}, f32[80,1024]{1,0:T(8,128)S(1)}) custom-call(s32[1]{0:T(128)} %bitcast.10.rep_ref, bf16[16,160,128]{2,1,0:T(8,128)(2,1)S(1)} %get-tuple-element.51.refs_0_, bf16[16,160,128]{2,1,0:T(8,128)(2,1)S(1)} %get-tuple-element.50.refs_1_, ...), custom_call_target="tpu_custom_call" | custom-call | flops 5368709120 | bytes 10737418 | tf_op jit(solution)/shard_map/grads/pallas_call | solution.py:303
  87.7 1.8 %collective-permute-start.2 = (f32[80,1024]{1,0:T(8,128)}, f32[80,1024]{1,0:T(8,128)S(1)}, u32[]{:S(2)}, u32[]{:S(2)}) collective-permute-start(f32[80,1024]{1,0:T(8,128)} %get-tuple-element.39), channel_id=1, source_target_pairs={{0,3},{1,0},{2,1},{3,2},{4,7},{5,4},{6,5},{7,6},{8,11},{9,8},{10,9... | collective-permute-start | bytes 983048 | tf_op jit(solution)/shard_map/ppermute | solution.py:321
  91.6 2.9 %collective-permute-start.7 = (f32[80,1024]{1,0:T(8,128)}, f32[80,1024]{1,0:T(8,128)}, u32[]{:S(2)}, u32[]{:S(2)}) collective-permute-start(f32[80,1024]{1,0:T(8,128)} %add.25), channel_id=1, source_target_pairs={{0,3},{1,0},{2,1},{3,2},{4,7},{5,4},{6,5},{7,6},{8,11},{9,8},{10,9... | collective-permute-start | bytes 983048 | tf_op jit(solution)/shard_map/ppermute | solution.py:321
  94.6 5.7 %grads.3 = (f32[80,1024]{1,0:T(8,128)S(1)}, f32[80,1024]{1,0:T(8,128)S(1)}) custom-call(s32[1]{0:T(128)} %bitcast.10.rep_ref, bf16[16,160,128]{2,1,0:T(8,128)(2,1)S(1)} %get-tuple-element.51.refs_0_, bf16[16,160,128]{2,1,0:T(8,128)(2,1)S(1)} %get-tuple-element.50.refs_1_, bf16[2,16,64,128]{3,2,1,0:T(8,128)(2,1)S(1)} %copy-done.10, ...), custom_call_target="tpu_custom_call" | custom-call | flops 2684354560 | bytes 5368709 | tf_op jit(solution)/shard_map/grads/pallas_call | solution.py:303
  101.7 1.4 %finish_pool.1 = f32[4,160,128]{2,1,0:T(8,128)} custom-call(f32[4,4,160,128]{3,2,1,0:T(8,128)S(1)} %bitcast.21, s32[4,128]{1,0:T(4,128)S(1)} %bitcast.23), custom_call_target="tpu_custom_call" | custom-call | tf_op jit(solution)/shard_map/finish_pool/pallas_call | solution.py:42
  103.1 4.2 %collective-permute-done.4.refs_2_ = f32[80,1024]{1,0:T(8,128)} collective-permute-done((f32[80,1024]{1,0:T(8,128)}, f32[80,1024]{1,0:T(8,128)}, u32[]{:S(2)}, u32[]{:S(2)}) %collective-permute-start.4) | collective-permute-done | bytes 327712 | tf_op jit(solution)/shard_map/ppermute | solution.py:321
  107.4 2.0 %join.1 = f32[160,1024]{1,0:T(8,128)} custom-call(f32[80,1024]{1,0:T(8,128)S(1)} %copy-done.1, f32[80,1024]{1,0:T(8,128)S(1)} %collective-permute-done.2.refs_1_, f32[80,1024]{1,0:T(8,128)} %collective-permute-done.4.refs_2_, f32[80,1024]{1,0:T(8,128)S(1)} %copy-done.3, f32[80,1024]{1,0:T(8,128)S(1)} %collective-permute-done.5.refs_4_, ...), custom_call_target="tpu_custom_call" | custom-call | tf_op jit(solution)/shard_map/join/pallas_call | solution.py:66
  (51 shorter events, 5.9 us)
Async XLA Ops:
  2.0 16.1 %all-to-all-start = ((s32[32,8,128]{2,1,0:T(8,128)}), s32[32,8,128]{2,1,0:T(8,128)S(1)}, u32[]{:S(2)}, u32[]{:S(2)}) async-start(s32[32,8,128]{2,1,0:T(8,128)} %bitcast.3), calls=%async_computation | async-start | bytes 262144 | tf_op jit(solution)/shard_map/all_to_all | solution.py:316
  19.3 26.5 %all-to-all-start.2 = ((f32[16,160,128]{2,1,0:T(8,128)}), f32[16,160,128]{2,1,0:T(8,128)}, u32[]{:S(2)}, u32[]{:S(2)}) async-start(f32[16,160,128]{2,1,0:T(8,128)} %bitcast.12), calls=%async_computation.2 | async-start | bytes 2621440 | tf_op jit(solution)/shard_map/all_to_all | solution.py:316
  37.7 38.3 %copy-start.5 = (bf16[2,16,64,128]{3,2,1,0:T(8,128)(2,1)}, bf16[2,16,64,128]{3,2,1,0:T(8,128)(2,1)S(1)}, u32[]{:S(2)}) copy-start(bf16[2,16,64,128]{3,2,1,0:T(8,128)(2,1)S(1)} %get-tuple-element.32.refs_10_) | copy-start | bytes 1572868
  37.7 21.2 %collective-permute-start = (f32[16,160,128]{2,1,0:T(8,128)}, f32[16,160,128]{2,1,0:T(8,128)}, u32[]{:S(2)}, u32[]{:S(2)}) collective-permute-start(f32[16,160,128]{2,1,0:T(8,128)} %get-tuple-element.25), channel_id=1, source_target_pairs={{0,4},{4,0},{1,5},{5,1},{2,6},{6,2},{3,7},{7,3},{8,12},{12,8},{9,1... | collective-permute-start | bytes 3932168 | tf_op jit(solution)/shard_map/ppermute | solution.py:321
  45.8 19.4 %collective-permute-start.1 = (f32[16,160,128]{2,1,0:T(8,128)}, f32[16,160,128]{2,1,0:T(8,128)}, u32[]{:S(2)}, u32[]{:S(2)}) collective-permute-start(f32[16,160,128]{2,1,0:T(8,128)} %all-to-all-done.2), channel_id=1, source_target_pairs={{0,4},{4,0},{1,5},{5,1},{2,6},{6,2},{3,7},{7,3},{8,12},{12,8},{9,1... | collective-permute-start | bytes 3932168 | tf_op jit(solution)/shard_map/ppermute | solution.py:321
  56.9 2.0 %copy-start.9 = (bf16[2,16,64,128]{3,2,1,0:T(8,128)(2,1)}, bf16[2,16,64,128]{3,2,1,0:T(8,128)(2,1)S(1)}, u32[]{:S(2)}) copy-start(bf16[2,16,64,128]{3,2,1,0:T(8,128)(2,1)S(1)} %get-tuple-element.26.refs_2_) | copy-start | bytes 1572868
  56.9 2.0 %copy-start.11 = (bf16[2,16,64,128]{3,2,1,0:T(8,128)(2,1)}, bf16[2,16,64,128]{3,2,1,0:T(8,128)(2,1)S(1)}, u32[]{:S(2)}) copy-start(bf16[2,16,64,128]{3,2,1,0:T(8,128)(2,1)S(1)} %get-tuple-element.27.refs_3_) | copy-start | bytes 1572868
  56.9 2.0 %copy-start.15 = (f32[8,16,128]{2,1,0:T(8,128)}, f32[8,16,128]{2,1,0:T(8,128)S(1)}, u32[]{:S(2)}) copy-start(f32[8,16,128]{2,1,0:T(8,128)S(1)} %get-tuple-element.31.refs_7_) | copy-start | bytes 196612
  56.9 19.1 %copy-start.13 = (f32[8,16,128]{2,1,0:T(8,128)}, f32[8,16,128]{2,1,0:T(8,128)S(1)}, u32[]{:S(2)}) copy-start(f32[8,16,128]{2,1,0:T(8,128)S(1)} %get-tuple-element.30.refs_6_) | copy-start | bytes 196612
  61.5 40.2 %all-to-all-start.1 = ((f32[16,160,128]{2,1,0:T(8,128)}), f32[16,160,128]{2,1,0:T(8,128)S(1)}, u32[]{:S(2)}, u32[]{:S(2)}) async-start(f32[16,160,128]{2,1,0:T(8,128)} %add.23), calls=%async_computation.1 | async-start | bytes 2621440 | tf_op jit(solution)/shard_map/all_to_all | solution.py:316
  65.2 1.7 %copy-start.8 = (bf16[2,16,64,128]{3,2,1,0:T(8,128)(2,1)S(1)}, bf16[2,16,64,128]{3,2,1,0:T(8,128)(2,1)}, u32[]{:S(2)}) copy-start(bf16[2,16,64,128]{3,2,1,0:T(8,128)(2,1)} %copy-done.7) | copy-start | bytes 1572868
  65.2 1.7 %copy-start.12 = (bf16[2,16,64,128]{3,2,1,0:T(8,128)(2,1)S(1)}, bf16[2,16,64,128]{3,2,1,0:T(8,128)(2,1)}, u32[]{:S(2)}) copy-start(bf16[2,16,64,128]{3,2,1,0:T(8,128)(2,1)} %copy-done.11) | copy-start | bytes 1572868
  65.2 1.7 %copy-start.16 = (f32[8,16,128]{2,1,0:T(8,128)S(1)}, f32[8,16,128]{2,1,0:T(8,128)}, u32[]{:S(2)}) copy-start(f32[8,16,128]{2,1,0:T(8,128)} %copy-done.15) | copy-start | bytes 196612
  72.7 17.1 %collective-permute-start.3 = (f32[80,1024]{1,0:T(8,128)S(1)}, f32[80,1024]{1,0:T(8,128)S(1)}, u32[]{:S(2)}, u32[]{:S(2)}) collective-permute-start(f32[80,1024]{1,0:T(8,128)S(1)} %get-tuple-element.41), channel_id=1, source_target_pairs={{0,1},{1,2},{2,3},{3,0},{4,5},{5,6},{6,7},{7,4},{8,9},{9,10},{10,1... | collective-permute-start | bytes 983048 | tf_op jit(solution)/shard_map/ppermute | solution.py:321
  74.3 16.6 %collective-permute-start.6 = (f32[80,1024]{1,0:T(8,128)S(1)}, f32[80,1024]{1,0:T(8,128)S(1)}, u32[]{:S(2)}, u32[]{:S(2)}) collective-permute-start(f32[80,1024]{1,0:T(8,128)S(1)} %get-tuple-element.45), channel_id=1, source_target_pairs={{0,3},{1,0},{2,1},{3,2},{4,7},{5,4},{6,5},{7,6},{8,11},{9,8},{10,9... | collective-permute-start | bytes 983048 | tf_op jit(solution)/shard_map/ppermute | solution.py:321
  87.7 6.8 %copy-start.6 = (bf16[2,16,64,128]{3,2,1,0:T(8,128)(2,1)S(1)}, bf16[2,16,64,128]{3,2,1,0:T(8,128)(2,1)}, u32[]{:S(2)}) copy-start(bf16[2,16,64,128]{3,2,1,0:T(8,128)(2,1)} %copy-done.5) | copy-start | bytes 1572868
  87.7 6.9 %copy-start.14 = (f32[8,16,128]{2,1,0:T(8,128)S(1)}, f32[8,16,128]{2,1,0:T(8,128)}, u32[]{:S(2)}) copy-start(f32[8,16,128]{2,1,0:T(8,128)} %copy-done.13) | copy-start | bytes 196612
  87.7 15.4 %collective-permute-start.2 = (f32[80,1024]{1,0:T(8,128)}, f32[80,1024]{1,0:T(8,128)S(1)}, u32[]{:S(2)}, u32[]{:S(2)}) collective-permute-start(f32[80,1024]{1,0:T(8,128)} %get-tuple-element.39), channel_id=1, source_target_pairs={{0,3},{1,0},{2,1},{3,2},{4,7},{5,4},{6,5},{7,6},{8,11},{9,8},{10,9... | collective-permute-start | bytes 983048 | tf_op jit(solution)/shard_map/ppermute | solution.py:321
  89.5 13.6 %collective-permute-start.5 = (f32[80,1024]{1,0:T(8,128)}, f32[80,1024]{1,0:T(8,128)S(1)}, u32[]{:S(2)}, u32[]{:S(2)}) collective-permute-start(f32[80,1024]{1,0:T(8,128)} %get-tuple-element.43), channel_id=1, source_target_pairs={{0,1},{1,2},{2,3},{3,0},{4,5},{5,6},{6,7},{7,4},{8,9},{9,10},{10,1... | collective-permute-start | bytes 983048 | tf_op jit(solution)/shard_map/ppermute | solution.py:321
  90.5 16.8 %collective-permute-start.4 = (f32[80,1024]{1,0:T(8,128)}, f32[80,1024]{1,0:T(8,128)}, u32[]{:S(2)}, u32[]{:S(2)}) collective-permute-start(f32[80,1024]{1,0:T(8,128)} %add.24), channel_id=1, source_target_pairs={{0,1},{1,2},{2,3},{3,0},{4,5},{5,6},{6,7},{7,4},{8,9},{9,10},{10,1... | collective-permute-start | bytes 983048 | tf_op jit(solution)/shard_map/ppermute | solution.py:321
  91.6 10.1 %copy-start.4 = (s32[128,4]{0,1:T(4,128)S(1)}, s32[128,4]{0,1:T(4,128)}, u32[]{:S(2)}) copy-start(s32[128,4]{0,1:T(4,128)} %param.6) | copy-start | bytes 6148
  91.6 15.7 %collective-permute-start.7 = (f32[80,1024]{1,0:T(8,128)}, f32[80,1024]{1,0:T(8,128)}, u32[]{:S(2)}, u32[]{:S(2)}) collective-permute-start(f32[80,1024]{1,0:T(8,128)} %add.25), channel_id=1, source_target_pairs={{0,3},{1,0},{2,1},{3,2},{4,7},{5,4},{6,5},{7,6},{8,11},{9,8},{10,9... | collective-permute-start | bytes 983048 | tf_op jit(solution)/shard_map/ppermute | solution.py:321
  101.7 5.7 %copy-start.1 = (f32[80,1024]{1,0:T(8,128)S(1)}, f32[80,1024]{1,0:T(8,128)}, u32[]{:S(2)}) copy-start(f32[80,1024]{1,0:T(8,128)} %copy-done) | copy-start | bytes 983044
  101.7 5.7 %copy-start.3 = (f32[80,1024]{1,0:T(8,128)S(1)}, f32[80,1024]{1,0:T(8,128)}, u32[]{:S(2)}) copy-start(f32[80,1024]{1,0:T(8,128)} %copy-done.2) | copy-start | bytes 983044
  (4 other events, 4.0 us)

commit v4 on v3

--- a/solution.py
+++ b/solution.py
@@ -172,16 +172,21 @@
     def _():
         deepest = make_keys(base_ref[0], rows_dev, ids_ref, key_low, key_high, key_count)
         deep_ref[0] = 0
-
-        @pl.when(jnp.max(deepest) > 2)
-        def _():
-            for s in range(sources):
-                def note(depth, carry, s=s):
-                    deep_ref[0] += 1
-                    deep_ref[deep_ref[0]] = s * DEPTHS + depth
-                    return carry
-
-                lax.fori_loop(2, jnp.max(deepest[s : s + 1]), note, 0)
+        source_of = lax.broadcasted_iota(I32, deepest.shape, 0)
+        code = jnp.where(deepest > 2, source_of * 16 + deepest, 0)
+
+        def note_all(top):
+            source = top // 16
+
+            def note(depth, carry):
+                deep_ref[0] += 1
+                deep_ref[deep_ref[0]] = source * DEPTHS + depth
+                return carry
+
+            lax.fori_loop(2, top % 16, note, 0)
+            return jnp.max(jnp.where(source_of < source, code, 0))
+
+        lax.while_loop(lambda top: top > 0, note_all, jnp.max(code))
 
         build(0)
 
@@ -207,7 +212,7 @@
         @pl.when(source // per_step == step)
         def _():
             extra = deep_layer(source, deep_ref[1 + entry] % DEPTHS, key_low, key_high, key_count)
-            wide = 512
+            wide = 1024
 
             def add(block, value):
                 tile = jnp.concatenate([counts_for(block * (wide // LOW) + h, [extra])
@@ -295,7 +300,7 @@
 
 def grads(rep, aheads, each, rows, own, other):
     sources, width, _ = own[0].shape
-    blk = 256
+    blk = 1024
     steps = rows // blk
     outs = [pl.BlockSpec((width // each, blk), lambda i, g=g: (0, jnp.clip(i - g * steps, 0, steps - 1)))
             for g in range(len(aheads)) for _ in range(each)]

time: 111 us -> 105 us (0.946)
  Pallas kernels: 48.6 us -> 40.4 us
  waiting for transfers between devices: 18.3 us -> 20.4 us
    pallas_call x3, Pallas kernels: 23.1 us -> 14.9 us  [grads(): pl.pallas_call(functools.partial(grad_kernel, blk, steps, aheads), grid=(...]
    ppermute x8, waiting for transfers between devices: 4.27 us -> 6.45 us  [shifted(): return lax.ppermute(x, axis, [(i, (i + by) % n) for i in range(n)])]
  transfers between devices with their start and end apart: 11 -> 11, of which waited for: 3 -> 4; matrix products, arithmetic and copies ran while one was open for 11% -> 11% of each run, Pallas kernels for 43% -> 37%
where the time goes in v4:
time: 105 us; the launch traced here: 103 us
  Pallas kernels  40.4 us (38%)
  starting transfers between devices  25.2 us (24%)
  waiting for transfers between devices  20.4 us (19%)
  other arithmetic  12.2 us (12%)
  local copies, waits for them, and re-layouts  4.26 us (4%)
    pallas_call x2, Pallas kernels, pool(): pl.pallas_call(functools.partial(pool_kernel, per_step), grid=(sources //...  22.1 us
    all_to_all x3, starting transfers between devices, to_all(): return lax.all_to_all(x, axis, split_axis=0, concat_axis=0, tiled=True)  16.4 us
    pallas_call x3, Pallas kernels, grads(): pl.pallas_call(functools.partial(grad_kernel, blk, steps, aheads), grid=(...  14.9 us
    all_to_all x3, waiting for transfers between devices, to_all(): return lax.all_to_all(x, axis, split_axis=0, concat_axis=0, tiled=True)  14 us
    ppermute x8, starting transfers between devices, shifted(): return lax.ppermute(x, axis, [(i, (i + by) % n) for i in range(n)])  8.86 us
    ppermute x8, waiting for transfers between devices, shifted(): return lax.ppermute(x, axis, [(i, (i + by) % n) for i in range(n)])  6.45 us
    convert_element_type x3, other arithmetic, two_parts(): return (high.astype(BF), (x - high).astype(BF))  5.74 us
    add x1, other arithmetic, inner(): kept + sent  2.54 us
  transfers between devices with their start and end apart: 11, of which 4 were waited for; matrix products, arithmetic and copies ran while one was open for 11% of the time, Pallas kernels for 37%

profile of v4, /device:TPU:0, one launch (start us, length us, event | category | flops | bytes accessed | tf_op | source)
XLA Modules:
  0.0 103.4 jit_solution(12064258090531408252)
XLA Ops:
  2.0 8.3 %all-to-all-start = ((s32[32,8,128]{2,1,0:T(8,128)}), s32[32,8,128]{2,1,0:T(8,128)S(1)}, u32[]{:S(2)}, u32[]{:S(2)}) async-start(s32[32,8,128]{2,1,0:T(8,128)} %bitcast.3), calls=%async_computation | async-start | bytes 262144 | tf_op jit(solution)/shard_map/all_to_all | solution.py:321
  11.0 1.0 bitcast_multiply_fusion
  12.0 6.1 %all-to-all-done = s32[32,8,128]{2,1,0:T(8,128)S(1)} async-done(((s32[32,8,128]{2,1,0:T(8,128)}), s32[32,8,128]{2,1,0:T(8,128)S(1)}, u32[]{:S(2)}, u32[]{:S(2)}) %all-to-all-start) | async-done | bytes 131104 | tf_op jit(solution)/shard_map/all_to_all | solution.py:321
  18.1 1.2 %broadcast_in_dim.17 = f32[4,4,160,128]{3,2,1,0:T(8,128)} broadcast(f32[4,160,128]{2,1,0:T(8,128)S(1)} %bitcast_multiply_fusion), dimensions={0,2,3} | broadcast | bytes 1638400 | tf_op jit(solution)/shard_map/broadcast_in_dim | solution.py:352
  19.3 4.4 %all-to-all-start.2 = ((f32[16,160,128]{2,1,0:T(8,128)}), f32[16,160,128]{2,1,0:T(8,128)}, u32[]{:S(2)}, u32[]{:S(2)}) async-start(f32[16,160,128]{2,1,0:T(8,128)} %bitcast.12), calls=%async_computation.2 | async-start | bytes 2621440 | tf_op jit(solution)/shard_map/all_to_all | solution.py:321
  23.7 2.2 %fusion = (bf16[160,4096]{1,0:T(8,128)(2,1)S(1)}, bf16[160,4096]{1,0:T(8,128)(2,1)S(1)}) fusion(f32[4096,160]{0,1:T(8,128)} %param.4), kind=kLoop, calls=%fused_computation.2 | loop fusion | flops 2621440 | bytes 5242880 | tf_op jit(solution)/shard_map/convert_element_type | solution.py:29
  25.9 11.0 %pool.3 = (f32[16,160,128]{2,1,0:T(8,128)}, bf16[2,16,64,128]{3,2,1,0:T(8,128)(2,1)S(1)}, bf16[2,16,64,128]{3,2,1,0:T(8,128)(2,1)S(1)}, s32[129]{0:T(256)S(1)}, ...) custom-call(s32[1]{0:T(128)} %bitcast.base_ref, ...), custom_call_target="tpu_custom_call" | custom-call | flops 5368709120 | bytes 10737418 | tf_op jit(solution)/shard_map/pool/pallas_call | solution.py:237
  36.9 0.8 copy-done.7
  37.9 7.9 %all-to-all-done.2 = f32[16,160,128]{2,1,0:T(8,128)} async-done(((f32[16,160,128]{2,1,0:T(8,128)}), f32[16,160,128]{2,1,0:T(8,128)}, u32[]{:S(2)}, u32[]{:S(2)}) %all-to-all-start.2) | async-done | bytes 1310752 | tf_op jit(solution)/shard_map/all_to_all | solution.py:321
  45.8 11.1 %pool.2 = (f32[16,160,128]{2,1,0:T(8,128)S(1)}, bf16[2,16,64,128]{3,2,1,0:T(8,128)(2,1)S(1)}, bf16[2,16,64,128]{3,2,1,0:T(8,128)(2,1)S(1)}, s32[129]{0:T(256)S(1...) custom-call(s32[1]{0:T(128)} %bitcast.base_ref, ...), custom_call_target="tpu_custom_call" | custom-call | flops 5368709120 | bytes 10737418 | tf_op jit(solution)/shard_map/pool/pallas_call | solution.py:237
  56.9 1.9 %fusion.1 = (bf16[16,160,128]{2,1,0:T(8,128)(2,1)S(1)}, bf16[16,160,128]{2,1,0:T(8,128)(2,1)S(1)}) fusion(f32[16,160,128]{2,1,0:T(8,128)} %all-to-all-done.2), kind=kLoop, calls=%fused_computation.7 | loop fusion | flops 1310720 | bytes 2621440 | tf_op jit(solution)/shard_map/convert_element_type | solution.py:29
  58.9 2.5 %add.23 = f32[16,160,128]{2,1,0:T(8,128)} add(f32[16,160,128]{2,1,0:T(8,128)S(1)} %get-tuple-element.24, f32[16,160,128]{2,1,0:T(8,128)} %collective-permute-done) | non-fusion elementwise | flops 327680 | bytes 3932160 | tf_op jit(solution)/shard_map/add | solution.py:360
  61.4 3.7 %all-to-all-start.1 = ((f32[16,160,128]{2,1,0:T(8,128)}), f32[16,160,128]{2,1,0:T(8,128)S(1)}, u32[]{:S(2)}, u32[]{:S(2)}) async-start(f32[16,160,128]{2,1,0:T(8,128)} %add.23), calls=%async_computation.1 | async-start | bytes 2621440 | tf_op jit(solution)/shard_map/all_to_all | solution.py:321
  65.2 1.6 %fusion.2 = (bf16[16,160,128]{2,1,0:T(8,128)(2,1)S(1)}, bf16[16,160,128]{2,1,0:T(8,128)(2,1)S(1)}) fusion(f32[16,160,128]{2,1,0:T(8,128)} %collective-permute-done.1), kind=kLoop, calls=%fused_computation.8 | loop fusion | flops 1310720 | bytes 2621440 | tf_op jit(solution)/shard_map/convert_element_type | solution.py:29
  66.9 3.6 %grads.5 = (f32[80,1024]{1,0:T(8,128)S(1)}, f32[80,1024]{1,0:T(8,128)S(1)}) custom-call(s32[1]{0:T(128)} %bitcast.10.rep_ref, bf16[16,160,128]{2,1,0:T(8,128)(2,1)S(1)} %get-tuple-element.51.refs_0_, bf16[16,160,128]{2,1,0:T(8,128)(2,1)S(1)} %get-tuple-element.50.refs_1_, bf16[2,16,64,128]{3,2,1,0:T(8,128)(2,1)S(1)} %copy-done.10, ...), custom_call_target="tpu_custom_call" | custom-call | flops 2684354560 | bytes 5368709 | tf_op jit(solution)/shard_map/grads/pallas_call | solution.py:308
  70.5 1.9 %collective-permute-start.3 = (f32[80,1024]{1,0:T(8,128)S(1)}, f32[80,1024]{1,0:T(8,128)S(1)}, u32[]{:S(2)}, u32[]{:S(2)}) collective-permute-start(f32[80,1024]{1,0:T(8,128)S(1)} %get-tuple-element.41), channel_id=1, source_target_pairs={{0,1},{1,2},{2,3},{3,0},{4,5},{5,6},{6,7},{7,4},{8,9},{9,10},{10,1... | collective-permute-start | bytes 983048 | tf_op jit(solution)/shard_map/ppermute | solution.py:326
  72.4 1.6 %collective-permute-start.6 = (f32[80,1024]{1,0:T(8,128)S(1)}, f32[80,1024]{1,0:T(8,128)S(1)}, u32[]{:S(2)}, u32[]{:S(2)}) collective-permute-start(f32[80,1024]{1,0:T(8,128)S(1)} %get-tuple-element.45), channel_id=1, source_target_pairs={{0,3},{1,0},{2,1},{3,2},{4,7},{5,4},{6,5},{7,6},{8,11},{9,8},{10,9... | collective-permute-start | bytes 983048 | tf_op jit(solution)/shard_map/ppermute | solution.py:326
  74.0 7.7 %grads.4 = (f32[80,1024]{1,0:T(8,128)S(1)}, f32[80,1024]{1,0:T(8,128)}, f32[80,1024]{1,0:T(8,128)}, f32[80,1024]{1,0:T(8,128)S(1)}) custom-call(s32[1]{0:T(128)} %bitcast.10.rep_ref, bf16[16,160,128]{2,1,0:T(8,128)(2,1)S(1)} %get-tuple-element.51.refs_0_, bf16[16,160,128]{2,1,0:T(8,128)(2,1)S(1)} %get-tuple-element.50.refs_1_, ...), custom_call_target="tpu_custom_call" | custom-call | flops 5368709120 | bytes 10737418 | tf_op jit(solution)/shard_map/grads/pallas_call | solution.py:308
  81.7 1.8 %collective-permute-start.2 = (f32[80,1024]{1,0:T(8,128)}, f32[80,1024]{1,0:T(8,128)S(1)}, u32[]{:S(2)}, u32[]{:S(2)}) collective-permute-start(f32[80,1024]{1,0:T(8,128)} %get-tuple-element.39), channel_id=1, source_target_pairs={{0,3},{1,0},{2,1},{3,2},{4,7},{5,4},{6,5},{7,6},{8,11},{9,8},{10,9... | collective-permute-start | bytes 983048 | tf_op jit(solution)/shard_map/ppermute | solution.py:326
  85.7 2.8 %collective-permute-start.7 = (f32[80,1024]{1,0:T(8,128)}, f32[80,1024]{1,0:T(8,128)}, u32[]{:S(2)}, u32[]{:S(2)}) collective-permute-start(f32[80,1024]{1,0:T(8,128)} %add.25), channel_id=1, source_target_pairs={{0,3},{1,0},{2,1},{3,2},{4,7},{5,4},{6,5},{7,6},{8,11},{9,8},{10,9... | collective-permute-start | bytes 983048 | tf_op jit(solution)/shard_map/ppermute | solution.py:326
  88.5 3.6 %grads.3 = (f32[80,1024]{1,0:T(8,128)S(1)}, f32[80,1024]{1,0:T(8,128)S(1)}) custom-call(s32[1]{0:T(128)} %bitcast.10.rep_ref, bf16[16,160,128]{2,1,0:T(8,128)(2,1)S(1)} %get-tuple-element.51.refs_0_, bf16[16,160,128]{2,1,0:T(8,128)(2,1)S(1)} %get-tuple-element.50.refs_1_, bf16[2,16,64,128]{3,2,1,0:T(8,128)(2,1)S(1)} %copy-done.10, ...), custom_call_target="tpu_custom_call" | custom-call | flops 2684354560 | bytes 5368709 | tf_op jit(solution)/shard_map/grads/pallas_call | solution.py:308
  93.6 1.4 %finish_pool.1 = f32[4,160,128]{2,1,0:T(8,128)} custom-call(f32[4,4,160,128]{3,2,1,0:T(8,128)S(1)} %bitcast.21, s32[4,128]{1,0:T(4,128)S(1)} %bitcast.23), custom_call_target="tpu_custom_call" | custom-call | tf_op jit(solution)/shard_map/finish_pool/pallas_call | solution.py:42
  95.6 5.8 %collective-permute-done.4.refs_2_ = f32[80,1024]{1,0:T(8,128)} collective-permute-done((f32[80,1024]{1,0:T(8,128)}, f32[80,1024]{1,0:T(8,128)}, u32[]{:S(2)}, u32[]{:S(2)}) %collective-permute-start.4) | collective-permute-done | bytes 327712 | tf_op jit(solution)/shard_map/ppermute | solution.py:326
  101.4 2.0 %join.1 = f32[160,1024]{1,0:T(8,128)} custom-call(f32[80,1024]{1,0:T(8,128)S(1)} %copy-done.1, f32[80,1024]{1,0:T(8,128)S(1)} %collective-permute-done.2.refs_1_, f32[80,1024]{1,0:T(8,128)} %collective-permute-done.4.refs_2_, f32[80,1024]{1,0:T(8,128)S(1)} %copy-done.3, f32[80,1024]{1,0:T(8,128)S(1)} %collective-permute-done.5.refs_4_, ...), custom_call_target="tpu_custom_call" | custom-call | tf_op jit(solution)/shard_map/join/pallas_call | solution.py:66
  (51 shorter events, 6.5 us)
Async XLA Ops:
  2.0 16.1 %all-to-all-start = ((s32[32,8,128]{2,1,0:T(8,128)}), s32[32,8,128]{2,1,0:T(8,128)S(1)}, u32[]{:S(2)}, u32[]{:S(2)}) async-start(s32[32,8,128]{2,1,0:T(8,128)} %bitcast.3), calls=%async_computation | async-start | bytes 262144 | tf_op jit(solution)/shard_map/all_to_all | solution.py:321
  19.3 26.5 %all-to-all-start.2 = ((f32[16,160,128]{2,1,0:T(8,128)}), f32[16,160,128]{2,1,0:T(8,128)}, u32[]{:S(2)}, u32[]{:S(2)}) async-start(f32[16,160,128]{2,1,0:T(8,128)} %bitcast.12), calls=%async_computation.2 | async-start | bytes 2621440 | tf_op jit(solution)/shard_map/all_to_all | solution.py:321
  37.7 36.3 %copy-start.5 = (bf16[2,16,64,128]{3,2,1,0:T(8,128)(2,1)}, bf16[2,16,64,128]{3,2,1,0:T(8,128)(2,1)S(1)}, u32[]{:S(2)}) copy-start(bf16[2,16,64,128]{3,2,1,0:T(8,128)(2,1)S(1)} %get-tuple-element.32.refs_10_) | copy-start | bytes 1572868
  37.7 21.1 %collective-permute-start = (f32[16,160,128]{2,1,0:T(8,128)}, f32[16,160,128]{2,1,0:T(8,128)}, u32[]{:S(2)}, u32[]{:S(2)}) collective-permute-start(f32[16,160,128]{2,1,0:T(8,128)} %get-tuple-element.25), channel_id=1, source_target_pairs={{0,4},{4,0},{1,5},{5,1},{2,6},{6,2},{3,7},{7,3},{8,12},{12,8},{9,1... | collective-permute-start | bytes 3932168 | tf_op jit(solution)/shard_map/ppermute | solution.py:326
  45.8 19.4 %collective-permute-start.1 = (f32[16,160,128]{2,1,0:T(8,128)}, f32[16,160,128]{2,1,0:T(8,128)}, u32[]{:S(2)}, u32[]{:S(2)}) collective-permute-start(f32[16,160,128]{2,1,0:T(8,128)} %all-to-all-done.2), channel_id=1, source_target_pairs={{0,4},{4,0},{1,5},{5,1},{2,6},{6,2},{3,7},{7,3},{8,12},{12,8},{9,1... | collective-permute-start | bytes 3932168 | tf_op jit(solution)/shard_map/ppermute | solution.py:326
  56.9 2.0 %copy-start.9 = (bf16[2,16,64,128]{3,2,1,0:T(8,128)(2,1)}, bf16[2,16,64,128]{3,2,1,0:T(8,128)(2,1)S(1)}, u32[]{:S(2)}) copy-start(bf16[2,16,64,128]{3,2,1,0:T(8,128)(2,1)S(1)} %get-tuple-element.26.refs_2_) | copy-start | bytes 1572868
  56.9 2.0 %copy-start.11 = (bf16[2,16,64,128]{3,2,1,0:T(8,128)(2,1)}, bf16[2,16,64,128]{3,2,1,0:T(8,128)(2,1)S(1)}, u32[]{:S(2)}) copy-start(bf16[2,16,64,128]{3,2,1,0:T(8,128)(2,1)S(1)} %get-tuple-element.27.refs_3_) | copy-start | bytes 1572868
  56.9 2.0 %copy-start.15 = (f32[8,16,128]{2,1,0:T(8,128)}, f32[8,16,128]{2,1,0:T(8,128)S(1)}, u32[]{:S(2)}) copy-start(f32[8,16,128]{2,1,0:T(8,128)S(1)} %get-tuple-element.31.refs_7_) | copy-start | bytes 196612
  56.9 17.1 %copy-start.13 = (f32[8,16,128]{2,1,0:T(8,128)}, f32[8,16,128]{2,1,0:T(8,128)S(1)}, u32[]{:S(2)}) copy-start(f32[8,16,128]{2,1,0:T(8,128)S(1)} %get-tuple-element.30.refs_6_) | copy-start | bytes 196612
  61.4 32.1 %all-to-all-start.1 = ((f32[16,160,128]{2,1,0:T(8,128)}), f32[16,160,128]{2,1,0:T(8,128)S(1)}, u32[]{:S(2)}, u32[]{:S(2)}) async-start(f32[16,160,128]{2,1,0:T(8,128)} %add.23), calls=%async_computation.1 | async-start | bytes 2621440 | tf_op jit(solution)/shard_map/all_to_all | solution.py:321
  65.1 1.7 %copy-start.8 = (bf16[2,16,64,128]{3,2,1,0:T(8,128)(2,1)S(1)}, bf16[2,16,64,128]{3,2,1,0:T(8,128)(2,1)}, u32[]{:S(2)}) copy-start(bf16[2,16,64,128]{3,2,1,0:T(8,128)(2,1)} %copy-done.7) | copy-start | bytes 1572868
  65.2 1.7 %copy-start.12 = (bf16[2,16,64,128]{3,2,1,0:T(8,128)(2,1)S(1)}, bf16[2,16,64,128]{3,2,1,0:T(8,128)(2,1)}, u32[]{:S(2)}) copy-start(bf16[2,16,64,128]{3,2,1,0:T(8,128)(2,1)} %copy-done.11) | copy-start | bytes 1572868
  65.2 1.7 %copy-start.16 = (f32[8,16,128]{2,1,0:T(8,128)S(1)}, f32[8,16,128]{2,1,0:T(8,128)}, u32[]{:S(2)}) copy-start(f32[8,16,128]{2,1,0:T(8,128)} %copy-done.15) | copy-start | bytes 196612
  70.5 13.2 %collective-permute-start.3 = (f32[80,1024]{1,0:T(8,128)S(1)}, f32[80,1024]{1,0:T(8,128)S(1)}, u32[]{:S(2)}, u32[]{:S(2)}) collective-permute-start(f32[80,1024]{1,0:T(8,128)S(1)} %get-tuple-element.41), channel_id=1, source_target_pairs={{0,1},{1,2},{2,3},{3,0},{4,5},{5,6},{6,7},{7,4},{8,9},{9,10},{10,1... | collective-permute-start | bytes 983048 | tf_op jit(solution)/shard_map/ppermute | solution.py:326
  72.4 12.5 %collective-permute-start.6 = (f32[80,1024]{1,0:T(8,128)S(1)}, f32[80,1024]{1,0:T(8,128)S(1)}, u32[]{:S(2)}, u32[]{:S(2)}) collective-permute-start(f32[80,1024]{1,0:T(8,128)S(1)} %get-tuple-element.45), channel_id=1, source_target_pairs={{0,3},{1,0},{2,1},{3,2},{4,7},{5,4},{6,5},{7,6},{8,11},{9,8},{10,9... | collective-permute-start | bytes 983048 | tf_op jit(solution)/shard_map/ppermute | solution.py:326
  81.7 6.8 %copy-start.6 = (bf16[2,16,64,128]{3,2,1,0:T(8,128)(2,1)S(1)}, bf16[2,16,64,128]{3,2,1,0:T(8,128)(2,1)}, u32[]{:S(2)}) copy-start(bf16[2,16,64,128]{3,2,1,0:T(8,128)(2,1)} %copy-done.5) | copy-start | bytes 1572868
  81.7 6.8 %copy-start.14 = (f32[8,16,128]{2,1,0:T(8,128)S(1)}, f32[8,16,128]{2,1,0:T(8,128)}, u32[]{:S(2)}) copy-start(f32[8,16,128]{2,1,0:T(8,128)} %copy-done.13) | copy-start | bytes 196612
  81.7 13.2 %collective-permute-start.2 = (f32[80,1024]{1,0:T(8,128)}, f32[80,1024]{1,0:T(8,128)S(1)}, u32[]{:S(2)}, u32[]{:S(2)}) collective-permute-start(f32[80,1024]{1,0:T(8,128)} %get-tuple-element.39), channel_id=1, source_target_pairs={{0,3},{1,0},{2,1},{3,2},{4,7},{5,4},{6,5},{7,6},{8,11},{9,8},{10,9... | collective-permute-start | bytes 983048 | tf_op jit(solution)/shard_map/ppermute | solution.py:326
  83.6 12.0 %collective-permute-start.5 = (f32[80,1024]{1,0:T(8,128)}, f32[80,1024]{1,0:T(8,128)S(1)}, u32[]{:S(2)}, u32[]{:S(2)}) collective-permute-start(f32[80,1024]{1,0:T(8,128)} %get-tuple-element.43), channel_id=1, source_target_pairs={{0,1},{1,2},{2,3},{3,0},{4,5},{5,6},{6,7},{7,4},{8,9},{9,10},{10,1... | collective-permute-start | bytes 983048 | tf_op jit(solution)/shard_map/ppermute | solution.py:326
  84.5 16.9 %collective-permute-start.4 = (f32[80,1024]{1,0:T(8,128)}, f32[80,1024]{1,0:T(8,128)}, u32[]{:S(2)}, u32[]{:S(2)}) collective-permute-start(f32[80,1024]{1,0:T(8,128)} %add.24), channel_id=1, source_target_pairs={{0,1},{1,2},{2,3},{3,0},{4,5},{5,6},{6,7},{7,4},{8,9},{9,10},{10,1... | collective-permute-start | bytes 983048 | tf_op jit(solution)/shard_map/ppermute | solution.py:326
  85.7 7.9 %copy-start.4 = (s32[128,4]{0,1:T(4,128)S(1)}, s32[128,4]{0,1:T(4,128)}, u32[]{:S(2)}) copy-start(s32[128,4]{0,1:T(4,128)} %param.6) | copy-start | bytes 6148
  85.7 15.7 %collective-permute-start.7 = (f32[80,1024]{1,0:T(8,128)}, f32[80,1024]{1,0:T(8,128)}, u32[]{:S(2)}, u32[]{:S(2)}) collective-permute-start(f32[80,1024]{1,0:T(8,128)} %add.25), channel_id=1, source_target_pairs={{0,3},{1,0},{2,1},{3,2},{4,7},{5,4},{6,5},{7,6},{8,11},{9,8},{10,9... | collective-permute-start | bytes 983048 | tf_op jit(solution)/shard_map/ppermute | solution.py:326
  93.6 7.8 %copy-start.1 = (f32[80,1024]{1,0:T(8,128)S(1)}, f32[80,1024]{1,0:T(8,128)}, u32[]{:S(2)}) copy-start(f32[80,1024]{1,0:T(8,128)} %copy-done) | copy-start | bytes 983044
  93.6 7.8 %copy-start.3 = (f32[80,1024]{1,0:T(8,128)S(1)}, f32[80,1024]{1,0:T(8,128)}, u32[]{:S(2)}) copy-start(f32[80,1024]{1,0:T(8,128)} %copy-done.2) | copy-start | bytes 983044
  (4 other events, 4.0 us)
